TPU v7x, 32 devices: a whole 2x2x4 slice. The times are simulated.
32 devices in a mesh: grp: 4 (over x, core), mem: 4 (over z), pair: 2 (over y).
Axes of the slice: x: 2, y: 2, z: 4, core: 2. Of those that a mesh axis runs over, the one named last changes fastest.
Arguments:
- voltages: bfloat16 [1024, 2, 71680], P(('grp', 'mem'), 'pair'), may hold values from -6 to 6
- gain_table: float32 [64, 2, 1024], P(None, None, 'mem'), may hold values from -4.2 to 4.2
- gain_index: int32 [1024, 2], replicated, may hold values from 0 to 63
- cylinder_map: int32 [1024], replicated, may hold values from 0 to 1023, each once
- delays: int32 [32, 1024], replicated, may hold values from 0 to 31
- chan_map: int32 [1024], replicated, may hold values from 0 to 1023, each once
Outputs:
- dedispersed: float32 [2, 512, 32, 32], P('pair', ('grp', 'mem'))
Inputs may be any that keep to these rules, and one draw needn't show every extreme that they name: `cylinder_map`: each of 0 to 1023 appears once. `chan_map`: each of 0 to 1023 appears once.
All inputs are finite; a program needn't handle non-finite values.
Results may differ from a plain program's by a relative error of at most 0.011.
Values may be sent and summed in bfloat16 or wider, within the bound.
A program may use at most 128 MiB of HBM per device.

v0:
```python
import functools
import math

import jax
import jax.numpy as jnp
from jax import lax
from jax.experimental import pallas as pl
from jax.experimental.pallas import tpu as pltpu
from jax.sharding import PartitionSpec as P

NFFT = 2048
CHANS = 1024
TAPS = 4
CYL = 4
NS = 256
FEEDS = 1024
BEAMS = 1024
TIMES = 32
TRIALS = 32
PEERS = ("grp", "mem")
LANES = 128


def pfb_window(tap_count, length):
    offsets = jnp.arange(tap_count * length, dtype=jnp.float32) + 0.5
    shaped = jnp.sinc((offsets - tap_count * length / 2.0) / length)
    taper_term = 0.5 - 0.5 * jnp.cos(offsets * (2.0 * math.pi / (tap_count * length)))
    return (shaped * taper_term).reshape(tap_count, length)


def turn(index, length):
    angles = (index % length).astype(jnp.float32) * (2.0 * math.pi / length)
    return lax.optimization_barrier((jnp.cos(angles), jnp.sin(angles)))


def times(a, b):
    return (a[0] * b[0] - a[1] * b[1], a[0] * b[1] + a[1] * b[0])


def channel_table(chan_of, quarter):
    chan = chan_of[None, :]
    high = turn(jnp.arange(16, dtype=jnp.int32)[:, None] * 128 * chan, NFFT)
    mid = turn(jnp.arange(16, dtype=jnp.int32)[:, None] * 8 * chan, NFFT)
    low = turn(jnp.arange(8, dtype=jnp.int32)[:, None] * chan + quarter[None, :] * (NFFT // 4), NFFT)
    upper = times([p[:, None, :] for p in high], [p[None, :, :] for p in mid])
    upper = lax.optimization_barrier(tuple(p.reshape(NFFT // 8, 1, -1) for p in upper))
    table = upper[0] * low[0][None] - upper[1] * low[1][None]
    return table.astype(jnp.bfloat16).reshape(NFFT, -1)


def beam_weights(cylinder_map):
    slots = jnp.arange(FEEDS, dtype=jnp.int32)
    hit = cylinder_map[:, None] == slots[None, :]
    slot_of = jnp.sum(jnp.where(hit, slots[:, None], 0), axis=0)
    cyl, pos = slot_of // NS, slot_of % NS
    e = jnp.arange(CYL, dtype=jnp.int32).reshape(CYL, 1, 1)
    hh = jnp.arange(16, dtype=jnp.int32).reshape(1, 16, 1)
    upper = turn(16 * pos * hh + (NS // CYL) * e * cyl, NS)
    a = jnp.arange(2, dtype=jnp.int32).reshape(2, 1, 1)
    hl = jnp.arange(8, dtype=jnp.int32).reshape(1, 8, 1)
    lower = turn(pos * (2 * hl + a), NS)
    real, imag = times(
        [p[None, :, :, None, :] for p in upper], [p[:, None, None, :, :] for p in lower]
    )
    return jnp.concatenate(
        [p.astype(jnp.bfloat16).reshape(BEAMS, FEEDS) for p in (real, imag)], axis=1
    )


BEAM_VMEM = 40
DFT_VMEM = 40
CHUNKS = (8, 20, 4)


def dft_kernel(frames, feeds, window_ref, volt_ref, table_ref, out_ref, framed_ref):
    @pl.when(pl.program_id(0) == 0)
    def _():
        for t in range(frames):
            total = volt_ref[:, t * NFFT : (t + 1) * NFFT].astype(jnp.float32) * window_ref[0:1, :]
            for j in range(1, TAPS):
                tap = volt_ref[:, (t + j) * NFFT : (t + j + 1) * NFFT].astype(jnp.float32)
                total = total + tap * window_ref[j : j + 1, :]
            framed_ref[t * feeds : (t + 1) * feeds, :] = total.astype(jnp.bfloat16)

    part = jnp.dot(framed_ref[...], table_ref[...], preferred_element_type=jnp.float32)
    part = (part * (1.0 / math.sqrt(NFFT))).astype(jnp.bfloat16)
    for i in range(out_ref.shape[0]):
        out_ref[i] = part[:, i * LANES : (i + 1) * LANES].reshape(frames, feeds, LANES)


def dft_stage(voltages, window, table, start, frames, peers):
    feeds = voltages.shape[0]
    length = (frames + TAPS - 1) * NFFT
    volt = lax.slice_in_dim(voltages, start * NFFT, start * NFFT + length, axis=2)
    volt = volt.reshape(feeds, length)
    width = table.shape[1] // peers
    if width != LANES:
        view = volt.reshape(feeds, frames + TAPS - 1, NFFT).astype(jnp.float32)
        framed = view[:, 0:frames] * window[0]
        for j in range(1, TAPS):
            framed = framed + view[:, j : j + frames] * window[j]
        rows = jnp.swapaxes(framed.astype(jnp.bfloat16), 0, 1).reshape(frames * feeds, NFFT)
        part = jnp.dot(rows, table, preferred_element_type=jnp.float32) * (1.0 / math.sqrt(NFFT))
        part = part.astype(jnp.bfloat16).reshape(frames, feeds, peers, width)
        return jnp.moveaxis(part, 2, 0)
    step = 4
    return pl.pallas_call(
        functools.partial(dft_kernel, frames, feeds),
        grid=(peers // step,),
        out_shape=jax.ShapeDtypeStruct((peers, frames, feeds, width), jnp.bfloat16),
        in_specs=[
            pl.BlockSpec((TAPS, NFFT), lambda i: (0, 0)),
            pl.BlockSpec((feeds, length), lambda i: (0, 0)),
            pl.BlockSpec((NFFT, step * width), lambda i: (0, i)),
        ],
        out_specs=pl.BlockSpec((step, frames, feeds, width), lambda i: (i, 0, 0, 0)),
        scratch_shapes=[pltpu.VMEM((frames * feeds, NFFT), jnp.bfloat16)],
        compiler_params=pltpu.CompilerParams(
            dimension_semantics=("arbitrary",), vmem_limit_bytes=DFT_VMEM * 1024 * 1024
        ),
    )(window, volt, table)


HIT = (TIMES - 1) / (TIMES * TIMES)
MISS = -1.0 / (TIMES * TIMES)


def beam_kernel(start, frames, chans, r_ref, ga_ref, gb_ref, w_ref, e_ref, *rest):
    acc_ref = rest[0] if len(rest) == 6 else None
    out_ref, even_ref, odd_ref, t_ref, p_ref = rest[-5:]
    width = 2 * chans
    lane = lax.broadcasted_iota(jnp.int32, (FEEDS, width), 1)
    sign = jnp.where(lane < chans, 1.0, -1.0)
    low = lax.broadcasted_iota(jnp.int32, (BEAMS, width), 1) < chans

    def calibrate(pair, x_ref):
        for u in range(2):
            i = 2 * pair + u
            volt = r_ref[:, i].reshape(FEEDS, width).astype(jnp.float32)
            cal = volt * ga_ref[...] + pltpu.roll(volt, chans, 1) * gb_ref[...]
            turned = pltpu.roll(cal, chans, 1) * sign
            cols = slice(u * width, (u + 1) * width)
            x_ref[0:FEEDS, cols] = cal.astype(jnp.bfloat16)
            x_ref[FEEDS : 2 * FEEDS, cols] = turned.astype(jnp.bfloat16)
            hit = e_ref[...] == start + i
            rows = pl.ds(pl.multiple_of(i * chans, chans), chans)
            t_ref[rows, :] = jnp.where(hit, HIT, MISS).astype(jnp.bfloat16)

    def form(pair, x_ref):
        beams = jnp.dot(w_ref[...], x_ref[...], preferred_element_type=jnp.float32)
        squares = beams * beams
        one, two = squares[:, :width], squares[:, width:]
        first = one + pltpu.roll(one, chans, 1)
        second = two + pltpu.roll(two, chans, 1)
        power = jnp.where(low, first, second) * (1.0 / FEEDS)
        p_ref[:, pl.ds(pl.multiple_of(pair * width, width), width)] = power.astype(jnp.bfloat16)

    pairs = frames // 2
    calibrate(0, even_ref)

    def body(k, carry):
        form(2 * k, even_ref)
        calibrate(2 * k + 1, odd_ref)
        form(2 * k + 1, odd_ref)
        calibrate(jnp.minimum(2 * k + 2, pairs - 1), even_ref)
        return carry

    lax.fori_loop(0, pairs // 2, body, 0)
    if pairs % 2:
        form(pairs - 1, even_ref)
    part = jnp.dot(p_ref[...], t_ref[...], preferred_element_type=jnp.float32)
    if acc_ref is not None:
        part = part + acc_ref[...]
    out_ref[...] = part.astype(out_ref.dtype)


def beam_stage(received, gains, weights, shift, start, acc):
    _, frames, _, width = received.shape
    chans = width // 2
    last = start + frames == TIMES
    held = jnp.bfloat16 if last else jnp.float32
    if width != LANES:
        volt = jnp.moveaxis(received, 1, 0).reshape(frames, FEEDS, 2, chans).astype(jnp.float32)
        ga, gb = (g.reshape(FEEDS, 2, chans) for g in gains)
        cal = (volt * ga + volt[:, :, ::-1] * gb).astype(jnp.bfloat16)
        turned = jnp.stack([cal[:, :, 1], -cal[:, :, 0]], axis=2)
        both = jnp.concatenate([cal, turned], axis=1)
        beams = jnp.einsum("bf,tfrc->btrc", weights, both, preferred_element_type=jnp.float32)
        power = jnp.sum(beams * beams, axis=2) * (1.0 / FEEDS)
        power = power.astype(jnp.bfloat16).reshape(BEAMS, frames * chans)
        frame = start + jnp.arange(frames, dtype=jnp.int32)[:, None, None]
        spread = jnp.where(shift[None] == frame, HIT, MISS).astype(jnp.bfloat16)
        spread = spread.reshape(frames * chans, -1)
        part = jnp.dot(power, spread, preferred_element_type=jnp.float32)
        return (part if acc is None else part + acc).astype(held)
    series = TRIALS * TIMES
    operands = (received, *gains, weights, shift) + (() if acc is None else (acc,))
    return pl.pallas_call(
        functools.partial(beam_kernel, start, frames, chans),
        out_shape=jax.ShapeDtypeStruct((BEAMS, series), held),
        in_specs=[pl.BlockSpec(memory_space=pltpu.VMEM)] * len(operands),
        out_specs=pl.BlockSpec(memory_space=pltpu.VMEM),
        scratch_shapes=[
            pltpu.VMEM((2 * FEEDS, 2 * width), jnp.bfloat16),
            pltpu.VMEM((2 * FEEDS, 2 * width), jnp.bfloat16),
            pltpu.VMEM((frames * chans, series), jnp.bfloat16),
            pltpu.VMEM((BEAMS, frames * chans), jnp.bfloat16),
        ],
        compiler_params=pltpu.CompilerParams(vmem_limit_bytes=BEAM_VMEM * 1024 * 1024),
    )(*operands)


def local(voltages, gain_table, gain_index, cylinder_map, delays, chan_map):
    feeds = voltages.shape[0]
    grp_count, mem_count = lax.axis_size("grp"), lax.axis_size("mem")
    peers = grp_count * mem_count
    chans = CHANS // peers
    grp, mem = lax.axis_index("grp"), lax.axis_index("mem")

    window = pfb_window(TAPS, NFFT)
    peer = jnp.arange(peers, dtype=jnp.int32)
    base = peer % mem_count * (CHANS // mem_count) + peer // mem_count * chans
    chan_of = base[:, None, None] + jnp.arange(chans, dtype=jnp.int32)[None, None, :]
    quarter = jnp.arange(2, dtype=jnp.int32)[None, :, None]
    chan_of, quarter = (
        jnp.broadcast_to(v, (peers, 2, chans)).reshape(-1) for v in (chan_of, quarter)
    )
    table = channel_table(chan_of, quarter)

    table = lax.optimization_barrier(table)
    starts = [sum(CHUNKS[:i]) for i in range(len(CHUNKS))]

    def exchange(spectra):
        return lax.all_to_all(spectra, PEERS, split_axis=0, concat_axis=0, tiled=True)

    spectra = [
        dft_stage(voltages, window, table, start, frames, peers)
        for start, frames in zip(starts, CHUNKS)
    ]
    received = [exchange(block) for block in spectra[:-1]]

    pairs = lax.axis_size("pair")
    cores = 2 if grp_count % 2 == 0 else 1
    owned = BEAMS // (pairs * peers)
    weights = beam_weights(cylinder_map)
    weights = weights.reshape(pairs, grp_count // cores, cores, mem_count * owned, 2 * FEEDS)
    weights = jnp.moveaxis(weights, 2, 0).reshape(BEAMS, 2 * FEEDS)
    gain_here = lax.dynamic_slice_in_dim(gain_table, grp * chans, chans, 2)
    gain_rows = gain_index[:, lax.axis_index("pair")]
    pick = gain_rows[:, None] == jnp.arange(gain_table.shape[0], dtype=jnp.int32)[None, :]
    gain_values = jnp.dot(
        pick.astype(jnp.float32),
        gain_here.reshape(gain_table.shape[0], 2 * chans),
        precision=lax.Precision.HIGHEST,
    )
    gain_real, gain_imag = gain_values[:, :chans], gain_values[:, chans:]
    gains = (
        jnp.concatenate([gain_real, gain_real], axis=1),
        jnp.concatenate([-gain_imag, gain_imag], axis=1),
    )

    first = mem * (CHANS // mem_count) + grp * chans
    freq = lax.dynamic_slice_in_dim(chan_map, first, chans, 0)
    column = jnp.arange(CHANS, dtype=jnp.int32)[:, None] == freq[None, :]
    delay = jnp.dot(
        delays.astype(jnp.bfloat16), column.astype(jnp.bfloat16), preferred_element_type=jnp.float32
    ).astype(jnp.int32)
    frame = jnp.arange(TIMES, dtype=jnp.int32)[None, None, :]
    shift = ((frame - delay.T[:, :, None]) % TIMES).reshape(chans, TRIALS * TIMES)

    part = None
    for i, start in enumerate(starts):
        if i == len(starts) - 1:
            last, part = lax.optimization_barrier((spectra[-1], held))
            received.append(exchange(last))
            part = beam_stage(received[i - 1], gains, weights, shift, starts[i - 1], part)
        if i == len(starts) - 2:
            held = part
            continue
        part = beam_stage(received[i], gains, weights, shift, start, part)

    series = TRIALS * TIMES
    groups = [[x * cores + c for c in range(cores)] for x in range(grp_count // cores)]
    part = part.reshape(cores, BEAMS // cores, series)
    part = lax.all_to_all(
        part, "grp", split_axis=0, concat_axis=0, axis_index_groups=groups, tiled=True
    )
    part = jnp.sum(part.astype(jnp.float32), axis=0).astype(jnp.bfloat16)
    part = part.reshape(pairs * peers // cores, owned, series)
    groups = [
        [
            (p * grp_count + x * cores + c) * mem_count + m
            for p in range(pairs)
            for x in range(grp_count // cores)
            for m in range(mem_count)
        ]
        for c in range(cores)
    ]
    part = lax.all_to_all(
        part, ("pair",) + PEERS, split_axis=0, concat_axis=0, axis_index_groups=groups, tiled=True
    )
    series = jnp.sum(part.astype(jnp.float32), axis=0)
    return series.reshape(1, owned, TRIALS, TIMES)


def solution(mesh):
    return jax.shard_map(
        local,
        mesh=mesh,
        in_specs=(P(PEERS, "pair", None), P(None, None, "mem"), P(), P(), P(), P()),
        out_specs=P("pair", PEERS, None, None),
        check_vma=False,
    )
```

profile of v0, /device:TPU:0, one launch (start us, length us, event | category | flops | bytes accessed | tf_op | source)
XLA Modules:
  0.0 277.0 jit_solution(776788660408650143)
XLA Ops:
  0.0 0.3 fusion.34.window_ref
  0.4 0.1 iota_add_fusion
  0.4 0.1 mul.578
  0.5 0.1 mul.601
  0.6 0.3 fusion.27
  0.9 1.1 fusion.25
  2.0 2.0 slice_bitcast_fusion.1.volt_ref
  4.0 0.6 multiply_add_fusion
  4.6 2.7 fusion.table_ref
  7.3 8.1 %shard_map.65 = bf16[16,8,64,128]{3,2,1,0:T(8,128)(2,1)} custom-call(f32[4,2048]{1,0:T(4,128)S(1)} %fusion.34.window_ref, bf16[64,22528]{1,0:T(8,128)(2,1)S(1)} %slice_bitcast_fusion.1.volt_ref, bf16[2048,2048]{1,0:T(8,128)(2,1)S(1)} %fusion.table_ref), custom_call_target="tpu_custom_call" | custom-call | tf_op jit(solution)/shard_map/pallas_call | solution.py:107
  15.4 3.3 %copy-done.2 = bf16[2048,2048]{1,0:T(8,128)(2,1)} copy-done((bf16[2048,2048]{1,0:T(8,128)(2,1)}, bf16[2048,2048]{1,0:T(8,128)(2,1)S(1)}, u32[]{:S(2)}) %copy-start.2) | copy-done | bytes 8388632
  18.7 7.4 %all-to-all-start = ((bf16[16,8,64,128]{3,2,1,0:T(8,128)(2,1)}), bf16[16,8,64,128]{3,2,1,0:T(8,128)(2,1)S(1)}, u32[]{:S(2)}, u32[]{:S(2)}) async-start(bf16[16,8,64,128]{3,2,1,0:T(8,128)(2,1)} %shard_map.65), calls=%async_computation | async-start | bytes 4194304 | tf_op jit(solution)/shard_map/all_to_all | solution.py:234
  26.1 3.1 %slice_bitcast_fusion.volt_ref = bf16[64,47104]{1,0:T(8,128)(2,1)S(1)} fusion(bf16[64,1,71680]{2,0,1:T(8,128)(2,1)} %param.6), kind=kLoop, calls=%fused_computation.2 | loop fusion | bytes 12058624 | tf_op jit(solution)/shard_map/reshape | solution.py:95
  29.2 17.3 %shard_map.67 = bf16[16,20,64,128]{3,2,1,0:T(8,128)(2,1)S(1)} custom-call(f32[4,2048]{1,0:T(4,128)S(1)} %fusion.34.window_ref, bf16[64,47104]{1,0:T(8,128)(2,1)S(1)} %slice_bitcast_fusion.volt_ref, bf16[2048,2048]{1,0:T(8,128)(2,1)} %copy-done.2), custom_call_target="tpu_custom_call" | custom-call | tf_op jit(solution)/shard_map/pallas_call | solution.py:107
  46.5 0.0 copy-start.7
  46.5 2.4 copy-done.7
  48.9 26.5 %all-to-all-done.r_ref = bf16[16,8,64,128]{3,2,1,0:T(8,128)(2,1)S(1)} async-done(((bf16[16,8,64,128]{3,2,1,0:T(8,128)(2,1)}), bf16[16,8,64,128]{3,2,1,0:T(8,128)(2,1)S(1)}, u32[]{:S(2)}, u32[]{:S(2)}) %all-to-all-start) | async-done | bytes 2097184 | tf_op jit(solution)/shard_map/all_to_all | solution.py:234
  75.4 4.8 %all-to-all-start.2 = ((bf16[16,20,64,128]{3,2,1,0:T(8,128)(2,1)}), bf16[16,20,64,128]{3,2,1,0:T(8,128)(2,1)}, u32[]{:S(2)}, u32[]{:S(2)}) async-start(bf16[16,20,64,128]{3,2,1,0:T(8,128)(2,1)} %copy-done.7), calls=%async_computation.2 | async-start | bytes 10485760 | tf_op jit(solution)/shard_map/all_to_all | solution.py:234
  80.2 0.1 sub.111
  80.3 0.1 constant_dynamic-slice_fusion
  80.4 0.1 reshape.369
  80.5 0.5 select_reduce_fusion
  81.1 0.3 fusion.35
  81.4 0.1 broadcast_multiply_fusion
  81.5 1.8 fusion.14
  83.3 0.8 dynamic_slice.11
  84.0 0.2 convolution_convert_fusion
  84.3 0.9 copy.19
  85.2 1.6 slice_bitcast_fusion.2.volt_ref
  86.8 3.4 %copy-done.3 = bf16[2048,2048]{1,0:T(8,128)(2,1)S(1)} copy-done((bf16[2048,2048]{1,0:T(8,128)(2,1)S(1)}, bf16[2048,2048]{1,0:T(8,128)(2,1)}, u32[]{:S(2)}) %copy-start.3) | copy-done | bytes 8388632
  90.2 4.3 %shard_map.64 = bf16[16,4,64,128]{3,2,1,0:T(8,128)(2,1)S(1)} custom-call(f32[4,2048]{1,0:T(4,128)S(1)} %fusion.34.window_ref, bf16[64,14336]{1,0:T(8,128)(2,1)S(1)} %slice_bitcast_fusion.2.volt_ref, bf16[2048,2048]{1,0:T(8,128)(2,1)S(1)} %copy-done.3), custom_call_target="tpu_custom_call" | custom-call | tf_op jit(solution)/shard_map/pallas_call | solution.py:107
  94.6 1.0 copy-done.12
  95.5 0.0 copy-done.16
  95.6 0.5 fusion.1
  96.0 0.2 slice_negate_fusion
  96.2 0.0 copy-start.13
  96.2 0.3 pad_maximum_fusion.1
  96.6 0.1 add_select_fusion.1.e_ref
  96.7 0.2 broadcast_bitcast_fusion
  97.0 0.3 mul.622
  97.3 0.0 copy-done.13
  97.3 0.3 mul.635
  97.5 1.1 subtract_convert_fusion.1
  98.7 0.4 pad_maximum_fusion
  99.1 7.7 %shard_map.66.rest_0_ = f32[1024,1024]{1,0:T(8,128)S(1)} custom-call(bf16[16,8,64,128]{3,2,1,0:T(8,128)(2,1)S(1)} %all-to-all-done.r_ref, f32[1024,128]{1,0:T(8,128)S(1)} %get-tuple-element.57.ga_ref, f32[1024,128]{1,0:T(8,128)S(1)} %get-tuple-element.58.gb_ref, bf16[1024,2048]{1,0:T(8,128)(2,1)S(1)} %bitcast.26, s32[64,1024]{1,0:T(8,128)S(1)} %add_select_fusion.1.e_ref), custom_call_target="tpu_custom_call" | custom-call | tf_op jit(solution)/shard_map/pallas_call | solution.py:198
  106.8 2.0 copy-done.4
  108.8 1.9 copy-done.8
  110.8 86.0 %all-to-all-done.2.r_ref = bf16[16,20,64,128]{3,2,1,0:T(8,128)(2,1)} async-done(((bf16[16,20,64,128]{3,2,1,0:T(8,128)(2,1)}), bf16[16,20,64,128]{3,2,1,0:T(8,128)(2,1)}, u32[]{:S(2)}, u32[]{:S(2)}) %all-to-all-start.2) | async-done | bytes 5242912 | tf_op jit(solution)/shard_map/all_to_all | solution.py:234
  196.7 3.9 %all-to-all-start.1 = ((bf16[16,4,64,128]{3,2,1,0:T(8,128)(2,1)}), bf16[16,4,64,128]{3,2,1,0:T(8,128)(2,1)S(1)}, u32[]{:S(2)}, u32[]{:S(2)}) async-start(bf16[16,4,64,128]{3,2,1,0:T(8,128)(2,1)} %copy-done.12), calls=%async_computation.1 | async-start | bytes 2097152 | tf_op jit(solution)/shard_map/all_to_all | solution.py:234
  200.6 0.0 copy-start.5
  200.7 2.2 copy-done.5
  202.8 2.2 copy-done.9
  205.0 20.6 %shard_map.68.rest_0_ = f32[1024,1024]{1,0:T(8,128)S(1)} custom-call(bf16[16,20,64,128]{3,2,1,0:T(8,128)(2,1)} %all-to-all-done.2.r_ref, f32[1024,128]{1,0:T(8,128)S(1)} %get-tuple-element.57.ga_ref, f32[1024,128]{1,0:T(8,128)S(1)} %get-tuple-element.58.gb_ref, bf16[1024,2048]{1,0:T(8,128)(2,1)S(1)} %bitcast.27, s32[64,1024]{1,0:T(8,128)S(1)} %add_select_fusion.1.e_ref, ...), custom_call_target="tpu_custom_call" | custom-call | tf_op jit(solution)/shard_map/pallas_call | solution.py:198
  225.7 1.9 copy-done.10
  227.6 0.0 all-to-all-done.1.r_ref
  227.6 2.2 copy-done.6
  229.8 2.2 copy-done.11
  232.0 3.5 %shard_map.69 = bf16[1024,1024]{1,0:T(8,128)(2,1)S(1)} custom-call(bf16[16,4,64,128]{3,2,1,0:T(8,128)(2,1)S(1)} %all-to-all-done.1.r_ref, f32[1024,128]{1,0:T(8,128)S(1)} %get-tuple-element.57.ga_ref, f32[1024,128]{1,0:T(8,128)S(1)} %get-tuple-element.58.gb_ref, bf16[1024,2048]{1,0:T(8,128)(2,1)S(1)} %bitcast.28, s32[64,1024]{1,0:T(8,128)S(1)} %add_select_fusion.1.e_ref, ...), custom_call_target="tpu_custom_call" | custom-call | tf_op jit(solution)/shard_map/pallas_call | solution.py:198
  235.5 0.0 copy-start.1
  235.5 5.5 %all_to_all.25 = bf16[2,512,1024]{2,1,0:T(8,128)(2,1)S(1)} all-to-all(bf16[2,512,1024]{2,1,0:T(8,128)(2,1)S(1)} %bitcast.29), channel_id=1, replica_groups={{0,8},{16,24},{1,9},{17,25},{2,10},{18,26},{3,11},{19,27},{4,12},{20,28..., dimensions={0} | all-to-all | bytes 4194304 | tf_op jit(solution)/shard_map/all_to_all | solution.py:285
  241.1 0.6 reduce_sum.31
  241.6 34.2 %all_to_all.26 = bf16[16,32,1024]{2,1,0:T(8,128)(2,1)S(1)} all-to-all(bf16[16,32,1024]{2,1,0:T(8,128)(2,1)S(1)} %bitcast.34), channel_id=1, replica_groups={{0,2,4,6,16,18,20,22,1,3,5,7,17,19,21,23},{8,10,12,14,24,26,28,30,9,11,..., dimensions={0} | all-to-all | bytes 2097152 | tf_op jit(solution)/shard_map/all_to_all | solution.py:299
  275.8 0.2 convert_reduce_fusion
  276.0 1.0 reshape.374
  (33 shorter events, 0.1 us)
Async XLA Ops:
  0.0 80.3 %copy-start = (f32[64,2,256]{2,1,0:T(2,128)S(1)}, f32[64,2,256]{2,1,0:T(2,128)}, u32[]{:S(2)}) copy-start(f32[64,2,256]{2,1,0:T(2,128)} %param.7) | copy-start | bytes 393220
  15.4 3.3 %copy-start.2 = (bf16[2048,2048]{1,0:T(8,128)(2,1)}, bf16[2048,2048]{1,0:T(8,128)(2,1)S(1)}, u32[]{:S(2)}) copy-start(bf16[2048,2048]{1,0:T(8,128)(2,1)S(1)} %fusion.table_ref) | copy-start | bytes 25165828
  18.7 56.7 %all-to-all-start = ((bf16[16,8,64,128]{3,2,1,0:T(8,128)(2,1)}), bf16[16,8,64,128]{3,2,1,0:T(8,128)(2,1)S(1)}, u32[]{:S(2)}, u32[]{:S(2)}) async-start(bf16[16,8,64,128]{3,2,1,0:T(8,128)(2,1)} %shard_map.65), calls=%async_computation | async-start | bytes 4194304 | tf_op jit(solution)/shard_map/all_to_all | solution.py:234
  46.5 2.4 copy-start.7
  48.8 31.7 %copy-start.18 = (s32[1024]{0:T(1024)S(1)}, s32[1024]{0:T(1024)}, u32[]{:S(2)}) copy-start(s32[1024]{0:T(1024)} %param.9) | copy-start | bytes 12292
  48.9 35.2 %copy-start.17 = (s32[32,1024]{1,0:T(8,128)S(1)}, s32[32,1024]{1,0:T(8,128)}, u32[]{:S(2)}) copy-start(s32[32,1024]{1,0:T(8,128)} %param.10) | copy-start | bytes 393220
  75.4 121.4 %all-to-all-start.2 = ((bf16[16,20,64,128]{3,2,1,0:T(8,128)(2,1)}), bf16[16,20,64,128]{3,2,1,0:T(8,128)(2,1)}, u32[]{:S(2)}, u32[]{:S(2)}) async-start(bf16[16,20,64,128]{3,2,1,0:T(8,128)(2,1)} %copy-done.7), calls=%async_computation.2 | async-start | bytes 10485760 | tf_op jit(solution)/shard_map/all_to_all | solution.py:234
  86.8 3.4 %copy-start.3 = (bf16[2048,2048]{1,0:T(8,128)(2,1)S(1)}, bf16[2048,2048]{1,0:T(8,128)(2,1)}, u32[]{:S(2)}) copy-start(bf16[2048,2048]{1,0:T(8,128)(2,1)} %copy-done.2) | copy-start | bytes 25165828
  90.2 5.3 %copy-start.16 = (s32[1024,2]{0,1:T(2,128)S(1)}, s32[1024,2]{0,1:T(2,128)}, u32[]{:S(2)}) copy-start(s32[1024,2]{0,1:T(2,128)} %param.8) | copy-start | bytes 24580
  94.6 1.0 copy-start.12
  95.5 1.1 copy-start.15
  95.5 1.4 copy-start.14
  96.2 1.0 copy-start.13
  106.8 2.0 copy-start.4
  108.8 2.0 copy-start.8
  196.7 30.9 %all-to-all-start.1 = ((bf16[16,4,64,128]{3,2,1,0:T(8,128)(2,1)}), bf16[16,4,64,128]{3,2,1,0:T(8,128)(2,1)S(1)}, u32[]{:S(2)}, u32[]{:S(2)}) async-start(bf16[16,4,64,128]{3,2,1,0:T(8,128)(2,1)} %copy-done.12), calls=%async_computation.1 | async-start | bytes 2097152 | tf_op jit(solution)/shard_map/all_to_all | solution.py:234
  200.6 2.2 copy-start.5
  202.8 2.2 copy-start.9
  225.7 2.0 copy-start.10
  227.6 2.2 copy-start.6
  229.8 2.2 copy-start.11
  235.5 41.5 %copy-start.1 = (f32[64,2,256]{2,1,0:T(2,128)S(1)}, f32[64,2,256]{2,1,0:T(2,128)}, u32[]{:S(2)}) copy-start(f32[64,2,256]{2,1,0:T(2,128)} %param.7) | copy-start | bytes 393220
where the time goes:
time: 278 us; the launch traced here: 277 us
  waiting for transfers between devices  112 us (40%)
  Pallas kernels  61.5 us (22%)
  blocking collectives  39.7 us (14%)
  local copies, waits for them, and re-layouts  35.3 us (13%)
  starting transfers between devices  16.1 us (6%)
  other arithmetic  10.8 us (4%)
    all_to_all x3, waiting for transfers between devices, exchange(): lax.all_to_all(spectra, PEERS, split_axis=0, concat_axis=0, tiled=True)  112 us
    all_to_all x1, blocking collectives, local(): lax.all_to_all(part, ('pair',) + PEERS, split_axis=0, concat_axis=0, axis...  34.2 us
    pallas_call x3, Pallas kernels, beam_stage(): pl.pallas_call(functools.partial(beam_kernel, start, frames, chans), out_...  31.8 us
    pallas_call x3, Pallas kernels, dft_stage(): pl.pallas_call(functools.partial(dft_kernel, frames, feeds), grid=(peers...  29.7 us
    unnamed x38, local copies, waits for them, and re-layouts  24.7 us
    all_to_all x3, starting transfers between devices, exchange(): lax.all_to_all(spectra, PEERS, split_axis=0, concat_axis=0, tiled=True)  16.1 us
    reshape x3, local copies, waits for them, and re-layouts, dft_stage(): volt = volt.reshape(feeds, length)  6.72 us
  transfers between devices with their start and end apart: 3, of which 2 were waited for; matrix products, arithmetic and copies ran while one was open for 5% of the time, Pallas kernels for 18%

commit v1 on v0

--- a/solution.py
+++ b/solution.py
@@ -302,10 +302,370 @@
     series = jnp.sum(part.astype(jnp.float32), axis=0)
     return series.reshape(1, owned, TRIALS, TIMES)
 
+GROUP = 4
+STEP = 2
+FUSED_VMEM = 62
+
+
+def fused_kernel(
+    sizes, window_ref, ga_ref, gb_ref, shift_ref, volt_hbm, table_hbm, weights_hbm, out_ref,
+    volt_ref, table_ref, w_ref, framed_ref, send_ref, recv_ref, x_ref, psend_ref, precv_ref,
+    t_ref, lhs_ref, acc_ref, zsend_ref, zrecv_ref,
+    head_sem, volt_sem, table_sem, w_sem, send_sem, recv_sem, own_sem,
+    psend_sem, precv_sem, pown_sem, zsend_sem, zrecv_sem,
+):
+    grp_count, mem_count, pairs, cores = sizes
+    peers = grp_count * mem_count
+    chips = peers // cores
+    feeds = volt_hbm.shape[0]
+    chans = LANES // 2
+    width = LANES
+    chunks = TIMES // GROUP
+    steps = GROUP // STEP
+    grp, mem, pair = (lax.axis_index(n) for n in ("grp", "mem", "pair"))
+    me = grp * mem_count + mem
+    across = pair * grp_count + grp
+    MESH = pl.DeviceIdType.MESH
+
+    def load(src, dst, sem):
+        return pltpu.make_async_copy(src, dst, sem)
+
+    head = (TAPS - 1) * NFFT
+    load(volt_hbm.at[:, 0:head], volt_ref.at[:, 0:head], head_sem).start()
+
+    def volt_copy(k):
+        cols = pl.ds(pl.multiple_of(head + k * (GROUP * NFFT), NFFT), GROUP * NFFT)
+        return load(volt_hbm.at[:, cols], volt_ref.at[:, cols], volt_sem.at[k])
+
+    def table_copy(chip):
+        cols = pl.ds(pl.multiple_of(chip * (cores * width), cores * width), cores * width)
+        return load(table_hbm.at[:, cols], table_ref.at[chip], table_sem.at[chip])
+
+    volt_copy(0).start()
+    for chip in range(chips):
+        table_copy(chip).start()
+    for k in range(1, chunks):
+        volt_copy(k).start()
+    load(weights_hbm, w_ref, w_sem).start()
+
+    barrier = pltpu.get_barrier_semaphore()
+    met = 0
+    for dg in range(grp_count):
+        for dm in range(mem_count):
+            for dp in range(pairs):
+                if (dg, dm, dp) == (0, 0, 0) or (dm != 0 and dp != 0):
+                    continue
+                there = {
+                    "grp": (grp + dg) % grp_count,
+                    "mem": (mem + dm) % mem_count,
+                    "pair": (pair + dp) % pairs,
+                }
+                pl.semaphore_signal(barrier, inc=1, device_id=there, device_id_type=MESH)
+                met += 1
+    pl.semaphore_wait(barrier, met)
+
+    acc_ref[...] = jnp.zeros_like(acc_ref)
+    load(volt_hbm.at[:, 0:head], volt_ref.at[:, 0:head], head_sem).wait()
+
+    def main_copy(q, g, m):
+        peer = g * mem_count + m
+        return pltpu.make_async_remote_copy(
+            src_ref=send_ref.at[q, peer],
+            dst_ref=recv_ref.at[q, me],
+            send_sem=send_sem.at[q],
+            recv_sem=recv_sem.at[q],
+            device_id={"grp": g, "mem": m},
+            device_id_type=MESH,
+        )
+
+    def own_copy(q):
+        return load(send_ref.at[q, me], recv_ref.at[q, me], own_sem.at[q])
+
+    x_here = grp // cores
+
+    def dft(k):
+        volt_copy(k).wait()
+        for t in range(GROUP):
+            def tap(j):
+                at = pl.multiple_of((k * GROUP + t + j) * NFFT, NFFT)
+                return volt_ref[:, pl.ds(at, NFFT)].astype(jnp.float32) * window_ref[j : j + 1, :]
+
+            total = tap(0)
+            for j in range(1, TAPS):
+                total = total + tap(j)
+            framed_ref[t * feeds : (t + 1) * feeds, :] = total.astype(jnp.bfloat16)
+
+        def tile(s, carry):
+            h = s // 2
+            far = (mem + 2) % 4 * ((3 - h) // 3) + (3 - mem) * (h % 3 % 2)
+            near = (mem + 1 - 2 * (mem % 2)) * (h % 3 // 2) + mem * (h // 3)
+            m = far + near
+            x = (x_here + s + 1) % 2
+            chip = x * mem_count + m
+
+            @pl.when(k == 0)
+            def _():
+                table_copy(chip).wait()
+
+            part = jnp.dot(framed_ref[...], table_ref[chip], preferred_element_type=jnp.float32)
+            part = (part * (1.0 / math.sqrt(NFFT))).astype(jnp.bfloat16)
+            for c in range(cores):
+                g = x * cores + c
+                peer = g * mem_count + m
+                for u in range(steps):
+                    q = k * steps + u
+                    rows = part[u * STEP * feeds : (u + 1) * STEP * feeds, c * width : (c + 1) * width]
+                    send_ref[q, peer] = rows.reshape(STEP, feeds, width)
+
+                @pl.when(peer != me)
+                def _():
+                    for u in range(steps):
+                        main_copy(k * steps + u, g, m).start()
+
+                @pl.when(peer == me)
+                def _():
+                    for u in range(steps):
+                        own_copy(k * steps + u).start()
+
+            return carry
+
+        lax.fori_loop(0, chips, tile, 0)
+
+    lane = lax.broadcasted_iota(jnp.int32, (FEEDS, width), 1)
+    sign = jnp.where(lane < chans, 1.0, -1.0)
+    low = lax.broadcasted_iota(jnp.int32, (BEAMS, width), 1) < chans
+    rows_each = BEAMS // (pairs * grp_count)
+
+    def arrived(q):
+        others = recv_ref.at[q, pl.ds(0, peers - 1)]
+        return load(others, others, recv_sem.at[q])
+
+    def left(q):
+        others = send_ref.at[q, pl.ds(0, peers - 1)]
+        return load(others, others, send_sem.at[q])
+
+    def power_copy(q, p, g):
+        d = p * grp_count + g
+        block = pl.ds(pl.multiple_of(d * rows_each, rows_each), rows_each)
+        return pltpu.make_async_remote_copy(
+            src_ref=psend_ref.at[q, block],
+            dst_ref=precv_ref.at[q, across],
+            send_sem=psend_sem.at[q],
+            recv_sem=precv_sem.at[q],
+            device_id={"pair": p, "grp": g},
+            device_id_type=MESH,
+        )
+
+    def power_own(q):
+        block = pl.ds(pl.multiple_of(across * rows_each, rows_each), rows_each)
+        return load(psend_ref.at[q, block], precv_ref.at[q, across], pown_sem.at[q])
+
+    others_count = pairs * grp_count - 1
+
+    def power_arrived(q):
+        others = precv_ref.at[q, pl.ds(0, others_count)]
+        return load(others, others, precv_sem.at[q])
+
+    def power_left(q):
+        others = psend_ref.at[q, pl.ds(0, others_count * rows_each)]
+        return load(others, others, psend_sem.at[q])
+
+    def beams(q):
+        arrived(q).wait()
+        own_copy(q).wait()
+        for u in range(STEP):
+            volt = recv_ref[q, :, u].reshape(FEEDS, width).astype(jnp.float32)
+            cal = volt * ga_ref[...] + pltpu.roll(volt, chans, 1) * gb_ref[...]
+            turned = pltpu.roll(cal, chans, 1) * sign
+            cols = slice(u * width, (u + 1) * width)
+            x_ref[0:FEEDS, cols] = cal.astype(jnp.bfloat16)
+            x_ref[FEEDS : 2 * FEEDS, cols] = turned.astype(jnp.bfloat16)
+        formed = jnp.dot(w_ref[...], x_ref[...], preferred_element_type=jnp.float32)
+        squares = formed * formed
+        one, two = squares[:, :width], squares[:, width:]
+        first = one + pltpu.roll(one, chans, 1)
+        second = two + pltpu.roll(two, chans, 1)
+        power = jnp.where(low, first, second) * (1.0 / FEEDS)
+        psend_ref[q] = power.astype(jnp.bfloat16)
+        for dp in range(pairs - 1, -1, -1):
+            for dg in range(grp_count - 1, -1, -1):
+                if dp == 0 and dg == 0:
+                    power_own(q).start()
+                else:
+                    power_copy(q, (pair + dp) % pairs, (grp + dg) % grp_count).start()
+
+    def dedisperse(q):
+        for s in range(grp_count):
+            for u in range(STEP):
+                hit = shift_ref[s * chans : (s + 1) * chans, :] == q * STEP + u
+                at = (s * STEP + u) * chans
+                t_ref[at : at + chans, :] = jnp.where(hit, HIT, MISS).astype(jnp.bfloat16)
+        power_arrived(q).wait()
+        power_own(q).wait()
+        for s in range(grp_count):
+            both = precv_ref[q, s].astype(jnp.float32)
+            for p in range(1, pairs):
+                both = both + precv_ref[q, p * grp_count + s].astype(jnp.float32)
+            lhs_ref[:, s * width : (s + 1) * width] = both.astype(jnp.bfloat16)
+        acc_ref[...] += jnp.dot(lhs_ref[...], t_ref[...], preferred_element_type=jnp.float32)
+
+    load(weights_hbm, w_ref, w_sem).wait()
+
+    def body(i, carry):
+        @pl.when(i < chunks)
+        def _():
+            dft(i)
+
+        @pl.when(i >= 3)
+        def _():
+            lax.fori_loop(0, steps, lambda u, c: (dedisperse((i - 3) * steps + u), c)[1], 0)
+
+        @pl.when(jnp.logical_and(i >= 2, i < chunks + 2))
+        def _():
+            lax.fori_loop(0, steps, lambda u, c: (beams((i - 2) * steps + u), c)[1], 0)
+
+        return carry
+
+    lax.fori_loop(0, chunks + 3, body, 0)
+
+    owned = rows_each // mem_count
+    zsend_ref[...] = acc_ref[...].astype(jnp.bfloat16)
+
+    def z_copy(d):
+        m = (mem + d) % mem_count
+        return pltpu.make_async_remote_copy(
+            src_ref=zsend_ref.at[pl.ds(pl.multiple_of(m * owned, owned), owned)],
+            dst_ref=zrecv_ref.at[d - 1],
+            send_sem=zsend_sem.at[d - 1],
+            recv_sem=zrecv_sem.at[d - 1],
+            device_id={"mem": m},
+            device_id_type=MESH,
+        )
+
+    for d in range(1, mem_count):
+        z_copy(d).start()
+
+    def drain(q, carry):
+        left(q).wait()
+        power_left(q).wait()
+        return carry
+
+    lax.fori_loop(0, chunks * steps, drain, 0)
+    total = acc_ref[pl.ds(pl.multiple_of(mem * owned, owned), owned), :]
+    for d in range(1, mem_count):
+        z_copy(d).wait()
+        total = total + zrecv_ref[d - 1].astype(jnp.float32)
+    out_ref[...] = total
+
+
+def fused_stage(sizes, window, gains, shift, voltages, table, weights):
+    grp_count, mem_count, pairs, cores = sizes
+    peers = grp_count * mem_count
+    chips = peers // cores
+    feeds, samples = voltages.shape
+    series = TRIALS * TIMES
+    count = TIMES // STEP
+    groups = pairs * grp_count
+    rows_each = BEAMS // groups
+    owned = rows_each // mem_count
+    bf16, f32 = jnp.bfloat16, jnp.float32
+    dma = pltpu.SemaphoreType.DMA
+    vmem = pl.BlockSpec(memory_space=pltpu.VMEM)
+    hbm = pl.BlockSpec(memory_space=pl.ANY)
+    return pl.pallas_call(
+        functools.partial(fused_kernel, sizes),
+        out_shape=jax.ShapeDtypeStruct((owned, series), f32),
+        in_specs=[vmem] * 4 + [hbm] * 3,
+        out_specs=vmem,
+        scratch_shapes=[
+            pltpu.VMEM((feeds, samples), bf16),
+            pltpu.VMEM((chips, NFFT, cores * LANES), bf16),
+            pltpu.VMEM((BEAMS, 2 * FEEDS), bf16),
+            pltpu.VMEM((GROUP * feeds, NFFT), bf16),
+            pltpu.VMEM((count, peers, STEP, feeds, LANES), bf16),
+            pltpu.VMEM((count, peers, STEP, feeds, LANES), bf16),
+            pltpu.VMEM((2 * FEEDS, STEP * LANES), bf16),
+            pltpu.VMEM((count, BEAMS, LANES), bf16),
+            pltpu.VMEM((count, groups, rows_each, LANES), bf16),
+            pltpu.VMEM((grp_count * LANES, series), bf16),
+            pltpu.VMEM((rows_each, grp_count * LANES), bf16),
+            pltpu.VMEM((rows_each, series), f32),
+            pltpu.VMEM((rows_each, series), bf16),
+            pltpu.VMEM((mem_count - 1, owned, series), bf16),
+            dma,
+            dma((TIMES // GROUP,)),
+            dma((chips,)),
+            dma,
+            dma((count,)),
+            dma((count,)),
+            dma((count,)),
+            dma((count,)),
+            dma((count,)),
+            dma((count,)),
+            dma((mem_count - 1,)),
+            dma((mem_count - 1,)),
+        ],
+        compiler_params=pltpu.CompilerParams(
+            collective_id=0, has_side_effects=True, vmem_limit_bytes=FUSED_VMEM * 1024 * 1024
+        ),
+    )(window, *gains, shift, voltages, table, weights)
+
+
+def local_fused(voltages, gain_table, gain_index, cylinder_map, delays, chan_map):
+    feeds = voltages.shape[0]
+    grp_count, mem_count = lax.axis_size("grp"), lax.axis_size("mem")
+    pairs, cores = lax.axis_size("pair"), 2
+    peers = grp_count * mem_count
+    chans = CHANS // peers
+    grp, mem = lax.axis_index("grp"), lax.axis_index("mem")
+    window = pfb_window(TAPS, NFFT)
+
+    peer = jnp.arange(peers, dtype=jnp.int32)
+    peer_grp = peer // (mem_count * cores) * cores + peer % cores
+    peer_mem = peer // cores % mem_count
+    base = peer_mem * (CHANS // mem_count) + peer_grp * chans
+    chan_of = base[:, None, None] + jnp.arange(chans, dtype=jnp.int32)[None, None, :]
+    quarter = jnp.arange(2, dtype=jnp.int32)[None, :, None]
+    chan_of, quarter = (
+        jnp.broadcast_to(v, (peers, 2, chans)).reshape(-1) for v in (chan_of, quarter)
+    )
+    table = channel_table(chan_of, quarter)
+    weights = beam_weights(cylinder_map)
+
+    gain_here = lax.dynamic_slice_in_dim(gain_table, grp * chans, chans, 2)
+    gain_rows = gain_index[:, lax.axis_index("pair")]
+    pick = gain_rows[:, None] == jnp.arange(gain_table.shape[0], dtype=jnp.int32)[None, :]
+    gain_values = jnp.dot(
+        pick.astype(jnp.float32),
+        gain_here.reshape(gain_table.shape[0], 2 * chans),
+        precision=lax.Precision.HIGHEST,
+    )
+    gain_real, gain_imag = gain_values[:, :chans], gain_values[:, chans:]
+    gains = (
+        jnp.concatenate([gain_real, gain_real], axis=1),
+        jnp.concatenate([-gain_imag, gain_imag], axis=1),
+    )
+
+    held = CHANS // mem_count
+    freq = lax.dynamic_slice_in_dim(chan_map, mem * held, held, 0)
+    column = jnp.arange(CHANS, dtype=jnp.int32)[:, None] == freq[None, :]
+    delay = jnp.dot(
+        delays.astype(jnp.bfloat16), column.astype(jnp.bfloat16), preferred_element_type=jnp.float32
+    ).astype(jnp.int32)
+    frame = jnp.arange(TIMES, dtype=jnp.int32)[None, None, :]
+    shift = ((frame - delay.T[:, :, None]) % TIMES).reshape(held, TRIALS * TIMES)
+
+    sizes = (grp_count, mem_count, pairs, cores)
+    series = fused_stage(
+        sizes, window, gains, shift, voltages.reshape(feeds, voltages.shape[2]), table, weights
+    )
+    return series.reshape(1, -1, TRIALS, TIMES)
+
 
 def solution(mesh):
+    shape = (mesh.shape["grp"], mesh.shape["mem"], mesh.shape["pair"])
     return jax.shard_map(
-        local,
+        local_fused if shape == (4, 4, 2) else local,
         mesh=mesh,
         in_specs=(P(PEERS, "pair", None), P(None, None, "mem"), P(), P(), P(), P()),
         out_specs=P("pair", PEERS, None, None),

time: 278 us -> 235 us (0.85)
  Pallas kernels: 61.5 us -> 211 us
  waiting for transfers between devices: 112 us -> 0 us
  blocking collectives: 39.7 us -> 0 us
  local copies, waits for them, and re-layouts: 35.3 us -> 3.54 us
  starting transfers between devices: 16.1 us -> 0 us
  other arithmetic: 10.8 us -> 19.2 us
    pallas_call x6 -> x1, Pallas kernels: 61.5 us -> 211 us  [fused_stage(): pl.pallas_call(functools.partial(fused_kernel, sizes), out_shape=jax.Shap...]
    all_to_all x3 -> x0, waiting for transfers between devices: 112 us -> none  [exchange(): lax.all_to_all(spectra, PEERS, split_axis=0, concat_axis=0, tiled=True)]
    all_to_all x2 -> x0, blocking collectives: 39.7 us -> none  [the longest x1 34.2 us: local(): lax.all_to_all(part, ('pair',) + PEERS, split_axis=0, concat_axis=0, axis...]
    unnamed x38 -> x8, local copies, waits for them, and re-layouts: 24.7 us -> 0.02 us
    all_to_all x3 -> x0, starting transfers between devices: 16.1 us -> none  [exchange(): lax.all_to_all(spectra, PEERS, split_axis=0, concat_axis=0, tiled=True)]
    reshape x5 -> x2, local copies, waits for them, and re-layouts: 7.79 us -> 1.98 us  [the longest x1 1.87 us: local_fused(): return series.reshape(1, -1, TRIALS, TIMES)]
    convert_element_type x1, other arithmetic: 2.68 us -> 6.37 us  [channel_table(): return table.astype(jnp.bfloat16).reshape(NFFT, -1)]
  transfers between devices with their start and end apart: 3 -> 0, of which waited for: 2 -> 0; matrix products, arithmetic and copies ran while one was open for 5% -> 0% of each run, Pallas kernels for 18% -> 0%
where the time goes in v1:
time: 235 us
  Pallas kernels  211 us (90%)
  other arithmetic  19.2 us (8%)
  local copies, waits for them, and re-layouts  3.54 us (2%)
    pallas_call x1, Pallas kernels, fused_stage(): pl.pallas_call(functools.partial(fused_kernel, sizes), out_shape=jax.Shap...  211 us
    convert_element_type x1, other arithmetic, channel_table(): return table.astype(jnp.bfloat16).reshape(NFFT, -1)  6.37 us

profile of v1, /device:TPU:0, one launch (start us, length us, event | category | flops | bytes accessed | tf_op | source)
XLA Modules:
  0.0 235.1 jit_solution(16010525473241746475)
XLA Ops:
  0.0 0.0 copy-start
  0.0 0.1 iota_add_fusion
  0.1 0.1 mul.529
  0.2 1.1 fusion.24
  1.3 2.0 multiply_add_fusion
  3.2 0.1 mul.552
  3.3 0.3 fusion.27
  3.6 0.0 copy-start.1
  3.6 6.4 %fusion.table_hbm = bf16[2048,2048]{1,0:T(8,128)(2,1)} fusion(f32[8,2048]{1,0:T(8,128)S(1)} %get-tuple-element.24, f32[256,2048]{1,0:T(8,128)S(1)} %bitcast.13, f32[8,2048]{1,0:T(8,128)S(1)} %get-tuple-element.22, f32[256,2048]{1,0:T(8,128)} %bitcast.14), kind=kLoop, calls=%fused_computation.1 | loop fusion | flops 16777216 | bytes 12713984 | tf_op jit(solution)/shard_map/convert_element_type | solution.py:48
  10.0 0.0 copy-start.3
  10.0 0.0 copy-done
  10.0 0.1 constant_dynamic-slice_fusion
  10.1 0.1 reshape.362
  10.2 0.0 copy-done.1
  10.2 0.5 fusion.3
  10.7 0.2 slice_negate_fusion
  10.9 1.3 pad_maximum_fusion.1
  12.2 0.0 copy-done.3
  12.2 0.5 select_reduce_fusion
  12.8 0.1 broadcast_multiply_fusion
  12.9 1.0 fusion.14
  13.9 0.3 fusion.35
  14.3 1.2 subtract_convert_fusion.1
  15.4 0.0 copy-start.2
  15.4 2.4 %pad_maximum_fusion.weights_hbm = bf16[1024,2048]{1,0:T(8,128)(2,1)} fusion(bf16[1024,1024]{1,0:T(8,128)(2,1)S(1)} %bitcast.16, bf16[1024,1024]{1,0:T(8,128)(2,1)S(1)} %bitcast.15), kind=kLoop, calls=%fused_computation.2 | loop fusion | flops 8388608 | bytes 8388608 | tf_op jit(solution)/shard_map/concatenate | solution.py:65
  17.8 0.8 dynamic_slice.11
  18.6 0.0 copy-done.2
  18.6 0.3 convolution_convert_fusion
  18.9 0.1 sub.104
  19.0 0.3 copy.15
  19.3 0.1 sub.102
  19.4 1.5 add_select_fusion.shift_ref
  20.9 0.9 fusion.34.window_ref
  21.8 211.4 %shard_map.64 = f32[32,1024]{1,0:T(8,128)} custom-call(f32[4,2048]{1,0:T(4,128)} %fusion.34.window_ref, f32[1024,128]{1,0:T(8,128)} %get-tuple-element.51.ga_ref, f32[1024,128]{1,0:T(8,128)} %get-tuple-element.52.gb_ref, s32[256,1024]{1,0:T(8,128)} %add_select_fusion.shift_ref, bf16[64,71680]{1,0:T(8,128)(2,1)} %bitcast.12, ...), custom_call_target="tpu_custom_call" | custom-call | tf_op jit(solution)/shard_map/pallas_call | solution.py:575
  233.2 1.9 reshape.364
  (11 shorter events, 0.1 us)
Async XLA Ops:
  0.0 10.0 %copy-start = (f32[64,2,256]{2,1,0:T(2,128)S(1)}, f32[64,2,256]{2,1,0:T(2,128)}, u32[]{:S(2)}) copy-start(f32[64,2,256]{2,1,0:T(2,128)} %param.7) | copy-start | bytes 393220
  3.6 6.6 %copy-start.1 = (s32[1024,2]{0,1:T(2,128)S(1)}, s32[1024,2]{0,1:T(2,128)}, u32[]{:S(2)}) copy-start(s32[1024,2]{0,1:T(2,128)} %param.8) | copy-start | bytes 24580
  10.0 2.3 copy-start.3
  15.4 3.2 %copy-start.2 = (s32[32,1024]{1,0:T(8,128)S(1)}, s32[32,1024]{1,0:T(8,128)}, u32[]{:S(2)}) copy-start(s32[32,1024]{1,0:T(8,128)} %param.10) | copy-start | bytes 393220

commit v2 on v1

--- a/solution.py
+++ b/solution.py
@@ -307,11 +307,146 @@
 FUSED_VMEM = 62
 
 
+def wave(index, length):
+    angles = (index & (length - 1)).astype(jnp.float32) * (2.0 * math.pi / length)
+    return jnp.cos(angles), jnp.sin(angles)
+
+
+def iota(shape, axis):
+    return lax.broadcasted_iota(jnp.int32, shape, axis)
+
+
+def fill_window(window_ref):
+    shape = (TAPS, NFFT)
+    offsets = (iota(shape, 0) * NFFT + iota(shape, 1)).astype(jnp.float32) + 0.5
+    arg = (offsets - TAPS * NFFT / 2.0) / NFFT * math.pi
+    taper = 0.5 - 0.5 * jnp.cos(offsets * (2.0 * math.pi / (TAPS * NFFT)))
+    window_ref[...] = jnp.sin(arg) / arg * taper
+
+
+def fill_waves(wave_ref, cores, chans):
+    shape = (8, cores * LANES)
+    lane = iota(shape, 1)
+    chan = lane // LANES * chans + lane % chans
+    quarter = lane % LANES // chans * (NFFT // 4)
+    start = wave(iota(shape, 0) * chan + quarter, NFFT)
+    wave_ref[0, 0:8, :], wave_ref[1, 0:8, :] = start
+    step = 8
+    while step < NFFT:
+        turn_real, turn_imag = (v[None] for v in wave(chan * step, NFFT))
+        real, imag = (wave_ref[r, 0:step, :].reshape(step // 8, *shape) for r in range(2))
+        rows = slice(step, 2 * step)
+        wave_ref[0, rows, :] = (real * turn_real - imag * turn_imag).reshape(step, shape[1])
+        wave_ref[1, rows, :] = (real * turn_imag + imag * turn_real).reshape(step, shape[1])
+        step *= 2
+
+
+def fill_table(table_ref, wave_ref, chip, first):
+    period = NFFT // LANES
+    shape = (period, table_ref.shape[2])
+    turn_real, turn_imag = (v[None] for v in wave(iota(shape, 0) * (first // LANES), period))
+    block = 256
+
+    def part(i, carry):
+        rows = pl.ds(pl.multiple_of(i * block, block), block)
+        real, imag = (wave_ref[r, rows, :].reshape(block // period, *shape) for r in range(2))
+        filled = (real * turn_real - imag * turn_imag).reshape(block, shape[1])
+        table_ref[chip, rows, :] = filled.astype(jnp.bfloat16)
+        return carry
+
+    lax.fori_loop(0, NFFT // block, part, 0)
+
+
+def fill_gains(gains_ref, gain_table_ref, gain_index_ref, grp, pair):
+    rows, _, held = gain_table_ref.shape
+    chans = LANES // 2
+    low = iota((rows, held), 1) < chans
+
+    def twice(values):
+        values = pltpu.roll(values, (held - grp * chans) % held, 1)
+        return jnp.where(low, values, pltpu.roll(values, chans, 1))[:, :LANES]
+
+    real = twice(gain_table_ref[:, 0, :])
+    imag = twice(gain_table_ref[:, 1, :])
+    imag = jnp.where(low[:, :LANES], -imag, imag)
+    left = jnp.concatenate([real, imag], axis=1)
+    index = gain_index_ref[pl.ds(pair, 1), :]
+    pick = jnp.where(iota((rows, index.shape[1]), 0) == index, 1.0, 0.0).astype(jnp.bfloat16)
+    total = None
+    for _ in range(3):
+        term = left.astype(jnp.bfloat16)
+        left = left - term.astype(jnp.float32)
+        picked = lax.dot_general(
+            pick, term, (((0,), (0,)), ((), ())), preferred_element_type=jnp.float32
+        )
+        total = picked if total is None else total + picked
+    gains_ref[...] = total
+
+
+def fill_shift(shift_ref, delays_ref, chan_map_ref, mem):
+    held, series = shift_ref.shape
+    freq = chan_map_ref[:, pl.ds(pl.multiple_of(mem * held, held), held)]
+    column = jnp.where(iota((CHANS, held), 0) == freq, 1.0, 0.0).astype(jnp.bfloat16)
+    known = delays_ref[...].astype(jnp.float32).astype(jnp.bfloat16)
+    delay = jnp.dot(known, column, preferred_element_type=jnp.float32).astype(jnp.bfloat16)
+    shape = (TRIALS, series)
+    spread = jnp.where(iota(shape, 1) // TIMES == iota(shape, 0), 1.0, 0.0).astype(jnp.bfloat16)
+    late = lax.dot_general(
+        delay, spread, (((0,), (0,)), ((), ())), preferred_element_type=jnp.float32
+    )
+    shift = (iota((held, series), 1) % TIMES).astype(jnp.float32) - late
+    shift_ref[...] = jnp.where(shift < 0.0, shift + TIMES, shift)
+
+
+def fill_weights(w_ref, hit_ref, upper_ref, cylinder_ref):
+    block = 128
+
+    def mark(i, carry):
+        at = pl.multiple_of(i * block, block)
+        hit = iota((block, FEEDS), 0) + at == cylinder_ref[...]
+        hit_ref[pl.ds(at, block), :] = jnp.where(hit, 1.0, 0.0).astype(jnp.bfloat16)
+        return carry
+
+    lax.fori_loop(0, FEEDS // block, mark, 0)
+    shape = (8, FEEDS)
+    row, slot = iota(shape, 0), iota(shape, 1)
+    digit = jnp.where(row == 0, slot // NS, jnp.where(row == 1, slot % NS // 16, slot % 16))
+    digit = digit.astype(jnp.float32).astype(jnp.bfloat16)
+    found = lax.dot_general(
+        digit, hit_ref[...], (((1,), (1,)), ((), ())), preferred_element_type=jnp.float32
+    )
+    cyl = found[0:1].astype(jnp.int32)
+    pos = (found[1:2] * 16.0 + found[2:3]).astype(jnp.int32)
+    shape = (CYL * 16, FEEDS)
+    row = iota(shape, 0)
+    upper = wave(16 * pos * (row % 16) + (NS // CYL) * cyl * (row // 16), NS)
+    upper_ref[0], upper_ref[1] = upper
+    shape = (8, FEEDS)
+    lower = [wave(pos * (2 * iota(shape, 0) + a), NS) for a in range(2)]
+
+    def pack(i, carry):
+        for a in range(2):
+            parts = [[], []]
+            for v in range(2):
+                at = pl.ds(i * 2 + v, 1)
+                real, imag = times((upper_ref[0, at, :], upper_ref[1, at, :]), lower[a])
+                parts[0].append(real)
+                parts[1].append(imag)
+            rows = pl.ds(pl.multiple_of(a * (BEAMS // 2) + i * 16, 16), 16)
+            for r in range(2):
+                both = jnp.concatenate(parts[r], axis=0).astype(jnp.bfloat16)
+                w_ref[rows, r * FEEDS : (r + 1) * FEEDS] = both
+        return carry
+
+    lax.fori_loop(0, CYL * 16 // 2, pack, 0)
+
+
 def fused_kernel(
-    sizes, window_ref, ga_ref, gb_ref, shift_ref, volt_hbm, table_hbm, weights_hbm, out_ref,
+    sizes, gain_table_ref, gain_index_ref, cylinder_ref, delays_ref, chan_map_ref, volt_hbm, out_ref,
     volt_ref, table_ref, w_ref, framed_ref, send_ref, recv_ref, x_ref, psend_ref, precv_ref,
     t_ref, lhs_ref, acc_ref, zsend_ref, zrecv_ref,
-    head_sem, volt_sem, table_sem, w_sem, send_sem, recv_sem, own_sem,
+    window_ref, wave_ref, gains_ref, shift_ref, hit_ref, upper_ref,
+    head_sem, volt_sem, send_sem, recv_sem, own_sem,
     psend_sem, precv_sem, pown_sem, zsend_sem, zrecv_sem,
 ):
     grp_count, mem_count, pairs, cores = sizes
@@ -337,16 +472,8 @@
         cols = pl.ds(pl.multiple_of(head + k * (GROUP * NFFT), NFFT), GROUP * NFFT)
         return load(volt_hbm.at[:, cols], volt_ref.at[:, cols], volt_sem.at[k])
 
-    def table_copy(chip):
-        cols = pl.ds(pl.multiple_of(chip * (cores * width), cores * width), cores * width)
-        return load(table_hbm.at[:, cols], table_ref.at[chip], table_sem.at[chip])
-
-    volt_copy(0).start()
-    for chip in range(chips):
-        table_copy(chip).start()
-    for k in range(1, chunks):
+    for k in range(chunks):
         volt_copy(k).start()
-    load(weights_hbm, w_ref, w_sem).start()
 
     barrier = pltpu.get_barrier_semaphore()
     met = 0
@@ -362,9 +489,10 @@
                 }
                 pl.semaphore_signal(barrier, inc=1, device_id=there, device_id_type=MESH)
                 met += 1
+    acc_ref[...] = jnp.zeros_like(acc_ref)
+    fill_window(window_ref)
+    fill_waves(wave_ref, cores, chans)
     pl.semaphore_wait(barrier, met)
-
-    acc_ref[...] = jnp.zeros_like(acc_ref)
     load(volt_hbm.at[:, 0:head], volt_ref.at[:, 0:head], head_sem).wait()
 
     def main_copy(q, g, m):
@@ -405,7 +533,8 @@
 
             @pl.when(k == 0)
             def _():
-                table_copy(chip).wait()
+                first = m * (CHANS // mem_count) + x * (cores * chans)
+                fill_table(table_ref, wave_ref, chip, first)
 
             part = jnp.dot(framed_ref[...], table_ref[chip], preferred_element_type=jnp.float32)
             part = (part * (1.0 / math.sqrt(NFFT))).astype(jnp.bfloat16)
@@ -475,7 +604,7 @@
         own_copy(q).wait()
         for u in range(STEP):
             volt = recv_ref[q, :, u].reshape(FEEDS, width).astype(jnp.float32)
-            cal = volt * ga_ref[...] + pltpu.roll(volt, chans, 1) * gb_ref[...]
+            cal = volt * gains_ref[:, :width] + pltpu.roll(volt, chans, 1) * gains_ref[:, width:]
             turned = pltpu.roll(cal, chans, 1) * sign
             cols = slice(u * width, (u + 1) * width)
             x_ref[0:FEEDS, cols] = cal.astype(jnp.bfloat16)
@@ -497,7 +626,8 @@
     def dedisperse(q):
         for s in range(grp_count):
             for u in range(STEP):
-                hit = shift_ref[s * chans : (s + 1) * chans, :] == q * STEP + u
+                frame = (q * STEP + u).astype(jnp.float32)
+                hit = shift_ref[s * chans : (s + 1) * chans, :] == frame
                 at = (s * STEP + u) * chans
                 t_ref[at : at + chans, :] = jnp.where(hit, HIT, MISS).astype(jnp.bfloat16)
         power_arrived(q).wait()
@@ -509,12 +639,16 @@
             lhs_ref[:, s * width : (s + 1) * width] = both.astype(jnp.bfloat16)
         acc_ref[...] += jnp.dot(lhs_ref[...], t_ref[...], preferred_element_type=jnp.float32)
 
-    load(weights_hbm, w_ref, w_sem).wait()
-
     def body(i, carry):
         @pl.when(i < chunks)
         def _():
             dft(i)
+
+        @pl.when(i == 1)
+        def _():
+            fill_gains(gains_ref, gain_table_ref, gain_index_ref, grp, pair)
+            fill_shift(shift_ref, delays_ref, chan_map_ref, mem)
+            fill_weights(w_ref, hit_ref, upper_ref, cylinder_ref)
 
         @pl.when(i >= 3)
         def _():
@@ -558,7 +692,7 @@
     out_ref[...] = total
 
 
-def fused_stage(sizes, window, gains, shift, voltages, table, weights):
+def fused_stage(sizes, gain_table, gain_index, cylinder_map, delays, chan_map, voltages):
     grp_count, mem_count, pairs, cores = sizes
     peers = grp_count * mem_count
     chips = peers // cores
@@ -571,11 +705,10 @@
     bf16, f32 = jnp.bfloat16, jnp.float32
     dma = pltpu.SemaphoreType.DMA
     vmem = pl.BlockSpec(memory_space=pltpu.VMEM)
-    hbm = pl.BlockSpec(memory_space=pl.ANY)
     return pl.pallas_call(
         functools.partial(fused_kernel, sizes),
         out_shape=jax.ShapeDtypeStruct((owned, series), f32),
-        in_specs=[vmem] * 4 + [hbm] * 3,
+        in_specs=[vmem] * 5 + [pl.BlockSpec(memory_space=pl.ANY)],
         out_specs=vmem,
         scratch_shapes=[
             pltpu.VMEM((feeds, samples), bf16),
@@ -592,10 +725,14 @@
             pltpu.VMEM((rows_each, series), f32),
             pltpu.VMEM((rows_each, series), bf16),
             pltpu.VMEM((mem_count - 1, owned, series), bf16),
+            pltpu.VMEM((TAPS, NFFT), f32),
+            pltpu.VMEM((2, NFFT, cores * LANES), f32),
+            pltpu.VMEM((FEEDS, 2 * LANES), f32),
+            pltpu.VMEM((CHANS // mem_count, series), f32),
+            pltpu.VMEM((FEEDS, FEEDS), bf16),
+            pltpu.VMEM((2, CYL * 16, FEEDS), f32),
             dma,
             dma((TIMES // GROUP,)),
-            dma((chips,)),
-            dma,
             dma((count,)),
             dma((count,)),
             dma((count,)),
@@ -608,56 +745,20 @@
         compiler_params=pltpu.CompilerParams(
             collective_id=0, has_side_effects=True, vmem_limit_bytes=FUSED_VMEM * 1024 * 1024
         ),
-    )(window, *gains, shift, voltages, table, weights)
+    )(gain_table, gain_index, cylinder_map, delays, chan_map, voltages)
 
 
 def local_fused(voltages, gain_table, gain_index, cylinder_map, delays, chan_map):
-    feeds = voltages.shape[0]
-    grp_count, mem_count = lax.axis_size("grp"), lax.axis_size("mem")
-    pairs, cores = lax.axis_size("pair"), 2
-    peers = grp_count * mem_count
-    chans = CHANS // peers
-    grp, mem = lax.axis_index("grp"), lax.axis_index("mem")
-    window = pfb_window(TAPS, NFFT)
-
-    peer = jnp.arange(peers, dtype=jnp.int32)
-    peer_grp = peer // (mem_count * cores) * cores + peer % cores
-    peer_mem = peer // cores % mem_count
-    base = peer_mem * (CHANS // mem_count) + peer_grp * chans
-    chan_of = base[:, None, None] + jnp.arange(chans, dtype=jnp.int32)[None, None, :]
-    quarter = jnp.arange(2, dtype=jnp.int32)[None, :, None]
-    chan_of, quarter = (
-        jnp.broadcast_to(v, (peers, 2, chans)).reshape(-1) for v in (chan_of, quarter)
-    )
-    table = channel_table(chan_of, quarter)
-    weights = beam_weights(cylinder_map)
-
-    gain_here = lax.dynamic_slice_in_dim(gain_table, grp * chans, chans, 2)
-    gain_rows = gain_index[:, lax.axis_index("pair")]
-    pick = gain_rows[:, None] == jnp.arange(gain_table.shape[0], dtype=jnp.int32)[None, :]
-    gain_values = jnp.dot(
-        pick.astype(jnp.float32),
-        gain_here.reshape(gain_table.shape[0], 2 * chans),
-        precision=lax.Precision.HIGHEST,
-    )
-    gain_real, gain_imag = gain_values[:, :chans], gain_values[:, chans:]
-    gains = (
-        jnp.concatenate([gain_real, gain_real], axis=1),
-        jnp.concatenate([-gain_imag, gain_imag], axis=1),
-    )
-
-    held = CHANS // mem_count
-    freq = lax.dynamic_slice_in_dim(chan_map, mem * held, held, 0)
-    column = jnp.arange(CHANS, dtype=jnp.int32)[:, None] == freq[None, :]
-    delay = jnp.dot(
-        delays.astype(jnp.bfloat16), column.astype(jnp.bfloat16), preferred_element_type=jnp.float32
-    ).astype(jnp.int32)
-    frame = jnp.arange(TIMES, dtype=jnp.int32)[None, None, :]
-    shift = ((frame - delay.T[:, :, None]) % TIMES).reshape(held, TRIALS * TIMES)
-
-    sizes = (grp_count, mem_count, pairs, cores)
+    feeds, _, samples = voltages.shape
+    sizes = (lax.axis_size("grp"), lax.axis_size("mem"), lax.axis_size("pair"), 2)
     series = fused_stage(
-        sizes, window, gains, shift, voltages.reshape(feeds, voltages.shape[2]), table, weights
+        sizes,
+        gain_table,
+        gain_index.T,
+        cylinder_map.reshape(1, FEEDS),
+        delays,
+        chan_map.reshape(1, CHANS),
+        voltages.reshape(feeds, samples),
     )
     return series.reshape(1, -1, TRIALS, TIMES)
 

time: 235 us -> 208 us (0.89)
  other arithmetic: 19.2 us -> 0 us
  Pallas kernels: 211 us -> 206 us
    convert_element_type x2 -> x0, other arithmetic: 7.53 us -> none  [the longest x1 6.37 us: channel_table(): return table.astype(jnp.bfloat16).reshape(NFFT, -1)]
    pallas_call x1, Pallas kernels: 211 us -> 206 us  [fused_stage(): pl.pallas_call(functools.partial(fused_kernel, sizes), out_shape=jax.Shap...]
    concatenate x2 -> x0, other arithmetic: 3.73 us -> none  [the longest x1 2.4 us: beam_weights(): jnp.concatenate([p.astype(jnp.bfloat16).reshape(BEAMS, FEEDS) for p in (r...]
    sin x4 -> x0, other arithmetic: 2.74 us -> none  [turn(): return lax.optimization_barrier((jnp.cos(angles), jnp.sin(angles)))]
where the time goes in v2:
time: 208 us
  Pallas kernels  206 us (99%)
    pallas_call x1, Pallas kernels, fused_stage(): pl.pallas_call(functools.partial(fused_kernel, sizes), out_shape=jax.Shap...  206 us

profile of v2, /device:TPU:0, one launch (start us, length us, event | category | flops | bytes accessed | tf_op | source)
XLA Modules:
  0.0 208.0 jit_solution(8055810004467285662)
XLA Ops:
  0.0 206.1 %shard_map.64 = f32[32,1024]{1,0:T(8,128)} custom-call(f32[64,2,256]{2,1,0:T(2,128)} %gain_table_ref.1, s32[2,1024]{1,0:T(2,128)} %bitcast.5, s32[1,1024]{1,0:T(1,128)} %bitcast.6, s32[32,1024]{1,0:T(8,128)} %delays_ref.1, s32[1,1024]{1,0:T(1,128)} %bitcast.7, bf16[64,71680]{1,0:T(8,128)(2,1)} %bitcast.4), custom_call_target="tpu_custom_call" | custom-call | tf_op jit(solution)/shard_map/pallas_call | solution.py:708
  206.1 1.9 reshape.15

commit v3 on v2

--- a/solution.py
+++ b/solution.py
@@ -383,19 +383,35 @@
     gains_ref[...] = total
 
 
-def fill_shift(shift_ref, delays_ref, chan_map_ref, mem):
+def fill_shifts(shift_ref, final_ref, delays_ref, chan_map_ref, mem):
     held, series = shift_ref.shape
-    freq = chan_map_ref[:, pl.ds(pl.multiple_of(mem * held, held), held)]
-    column = jnp.where(iota((CHANS, held), 0) == freq, 1.0, 0.0).astype(jnp.bfloat16)
     known = delays_ref[...].astype(jnp.float32).astype(jnp.bfloat16)
-    delay = jnp.dot(known, column, preferred_element_type=jnp.float32).astype(jnp.bfloat16)
     shape = (TRIALS, series)
     spread = jnp.where(iota(shape, 1) // TIMES == iota(shape, 0), 1.0, 0.0).astype(jnp.bfloat16)
-    late = lax.dot_general(
-        delay, spread, (((0,), (0,)), ((), ())), preferred_element_type=jnp.float32
-    )
-    shift = (iota((held, series), 1) % TIMES).astype(jnp.float32) - late
-    shift_ref[...] = jnp.where(shift < 0.0, shift + TIMES, shift)
+    frame = (iota((held, series), 1) % TIMES).astype(jnp.float32)
+
+    def some(m, carry):
+        rows = pl.ds(pl.multiple_of(m * held, held), held)
+        column = jnp.where(iota((CHANS, held), 0) == chan_map_ref[:, rows], 1.0, 0.0)
+        delay = jnp.dot(known, column.astype(jnp.bfloat16), preferred_element_type=jnp.float32)
+        late = lax.dot_general(
+            delay.astype(jnp.bfloat16),
+            spread,
+            (((0,), (0,)), ((), ())),
+            preferred_element_type=jnp.float32,
+        )
+        shift = frame - late
+        shift = jnp.where(shift < 0.0, shift + TIMES, shift)
+        hit = shift == float(TIMES - 1)
+        final_ref[rows, :] = jnp.where(hit, HIT, MISS).astype(jnp.bfloat16)
+
+        @pl.when(m == mem)
+        def _():
+            shift_ref[...] = shift
+
+        return carry
+
+    lax.fori_loop(0, CHANS // held, some, 0)
 
 
 def fill_weights(w_ref, hit_ref, upper_ref, cylinder_ref):
@@ -445,9 +461,9 @@
     sizes, gain_table_ref, gain_index_ref, cylinder_ref, delays_ref, chan_map_ref, volt_hbm, out_ref,
     volt_ref, table_ref, w_ref, framed_ref, send_ref, recv_ref, x_ref, psend_ref, precv_ref,
     t_ref, lhs_ref, acc_ref, zsend_ref, zrecv_ref,
-    window_ref, wave_ref, gains_ref, shift_ref, hit_ref, upper_ref,
+    window_ref, wave_ref, gains_ref, shift_ref, hit_ref, upper_ref, part_ref, parts_ref,
     head_sem, volt_sem, send_sem, recv_sem, own_sem,
-    psend_sem, precv_sem, pown_sem, zsend_sem, zrecv_sem,
+    psend_sem, precv_sem, pown_sem, zsend_sem, zrecv_sem, lsend_sem, lrecv_sem,
 ):
     grp_count, mem_count, pairs, cores = sizes
     peers = grp_count * mem_count
@@ -457,6 +473,7 @@
     width = LANES
     chunks = TIMES // GROUP
     steps = GROUP // STEP
+    last = TIMES // STEP - 1
     grp, mem, pair = (lax.axis_index(n) for n in ("grp", "mem", "pair"))
     me = grp * mem_count + mem
     across = pair * grp_count + grp
@@ -492,22 +509,48 @@
     acc_ref[...] = jnp.zeros_like(acc_ref)
     fill_window(window_ref)
     fill_waves(wave_ref, cores, chans)
-    pl.semaphore_wait(barrier, met)
     load(volt_hbm.at[:, 0:head], volt_ref.at[:, 0:head], head_sem).wait()
 
-    def main_copy(q, g, m):
+    def spectra_copy(q, at, g, m):
         peer = g * mem_count + m
         return pltpu.make_async_remote_copy(
-            src_ref=send_ref.at[q, peer],
-            dst_ref=recv_ref.at[q, me],
+            src_ref=send_ref.at[(at[0], peer) + at[1:]],
+            dst_ref=recv_ref.at[(at[0], me) + at[1:]],
             send_sem=send_sem.at[q],
             recv_sem=recv_sem.at[q],
             device_id={"grp": g, "mem": m},
             device_id_type=MESH,
         )
 
-    def own_copy(q):
-        return load(send_ref.at[q, me], recv_ref.at[q, me], own_sem.at[q])
+    def own_copy(q, at):
+        own = (at[0], me) + at[1:]
+        return load(send_ref.at[own], recv_ref.at[own], own_sem.at[q])
+
+    def post(q, at, g, m):
+        own = jnp.logical_and(g == grp, m == mem)
+
+        @pl.when(jnp.logical_not(own))
+        def _():
+            spectra_copy(q, at, g, m).start()
+
+        @pl.when(own)
+        def _():
+            own_copy(q, at).start()
+
+    def place(s):
+        h = s // 2
+        far = (mem + 2) % 4 * ((3 - h) // 3) + (3 - mem) * (h % 3 % 2)
+        near = (mem + 1 - 2 * (mem % 2)) * (h % 3 // 2) + mem * (h // 3)
+        return (x_here + s + 1) % 2, far + near
+
+    def post_all(q, at):
+        def some(s, carry):
+            x, m = place(s)
+            for c in range(cores):
+                post(q, at, x * cores + c, m)
+            return carry
+
+        lax.fori_loop(0, chips, some, 0)
 
     x_here = grp // cores
 
@@ -524,11 +567,7 @@
             framed_ref[t * feeds : (t + 1) * feeds, :] = total.astype(jnp.bfloat16)
 
         def tile(s, carry):
-            h = s // 2
-            far = (mem + 2) % 4 * ((3 - h) // 3) + (3 - mem) * (h % 3 % 2)
-            near = (mem + 1 - 2 * (mem % 2)) * (h % 3 // 2) + mem * (h // 3)
-            m = far + near
-            x = (x_here + s + 1) % 2
+            x, m = place(s)
             chip = x * mem_count + m
 
             @pl.when(k == 0)
@@ -539,89 +578,161 @@
             part = jnp.dot(framed_ref[...], table_ref[chip], preferred_element_type=jnp.float32)
             part = (part * (1.0 / math.sqrt(NFFT))).astype(jnp.bfloat16)
             for c in range(cores):
-                g = x * cores + c
-                peer = g * mem_count + m
+                peer = (x * cores + c) * mem_count + m
                 for u in range(steps):
-                    q = k * steps + u
                     rows = part[u * STEP * feeds : (u + 1) * STEP * feeds, c * width : (c + 1) * width]
-                    send_ref[q, peer] = rows.reshape(STEP, feeds, width)
-
-                @pl.when(peer != me)
-                def _():
+                    send_ref[k * steps + u, peer] = rows.reshape(STEP, feeds, width)
+
+            @pl.when(jnp.logical_and(k == 0, s == 0))
+            def _():
+                pl.semaphore_wait(barrier, met)
+
+            @pl.when(k == 0)
+            def _():
+                for c in range(cores):
                     for u in range(steps):
-                        main_copy(k * steps + u, g, m).start()
-
-                @pl.when(peer == me)
-                def _():
-                    for u in range(steps):
-                        own_copy(k * steps + u).start()
+                        post(u, (u,), x * cores + c, m)
 
             return carry
 
         lax.fori_loop(0, chips, tile, 0)
+
+        @pl.when(jnp.logical_and(k > 0, k < chunks - 1))
+        def _():
+            for u in range(steps):
+                post_all(k * steps + u, (k * steps + u,))
+
+        @pl.when(k == chunks - 1)
+        def _():
+            for u in range(steps - 1):
+                post_all(k * steps + u, (k * steps + u,))
+            for u in range(STEP):
+                post_all(last + u, (last, u))
 
     lane = lax.broadcasted_iota(jnp.int32, (FEEDS, width), 1)
     sign = jnp.where(lane < chans, 1.0, -1.0)
-    low = lax.broadcasted_iota(jnp.int32, (BEAMS, width), 1) < chans
     rows_each = BEAMS // (pairs * grp_count)
-
-    def arrived(q):
-        others = recv_ref.at[q, pl.ds(0, peers - 1)]
+    half = BEAMS // pairs
+    low = iota((half, width), 1) < chans
+    owned = rows_each // mem_count
+
+    def arrived(q, at):
+        others = recv_ref.at[(at[0], pl.ds(0, peers - 1)) + at[1:]]
         return load(others, others, recv_sem.at[q])
 
-    def left(q):
-        others = send_ref.at[q, pl.ds(0, peers - 1)]
+    def left(q, at):
+        others = send_ref.at[(at[0], pl.ds(0, peers - 1)) + at[1:]]
         return load(others, others, send_sem.at[q])
 
-    def power_copy(q, p, g):
-        d = p * grp_count + g
-        block = pl.ds(pl.multiple_of(d * rows_each, rows_each), rows_each)
+    others_count = pairs * grp_count - 1
+
+    def power_copy(q, src, dst, p, g):
         return pltpu.make_async_remote_copy(
-            src_ref=psend_ref.at[q, block],
-            dst_ref=precv_ref.at[q, across],
+            src_ref=src,
+            dst_ref=dst,
             send_sem=psend_sem.at[q],
             recv_sem=precv_sem.at[q],
             device_id={"pair": p, "grp": g},
             device_id_type=MESH,
         )
 
-    def power_own(q):
-        block = pl.ds(pl.multiple_of(across * rows_each, rows_each), rows_each)
-        return load(psend_ref.at[q, block], precv_ref.at[q, across], pown_sem.at[q])
-
-    others_count = pairs * grp_count - 1
-
-    def power_arrived(q):
-        others = precv_ref.at[q, pl.ds(0, others_count)]
-        return load(others, others, precv_sem.at[q])
-
-    def power_left(q):
-        others = psend_ref.at[q, pl.ds(0, others_count * rows_each)]
-        return load(others, others, psend_sem.at[q])
+    def power_from(q, d, u, single):
+        size = rows_each // 2 if single else rows_each
+        at = u * (half if single else 0) + d * size
+        return psend_ref.at[q, pl.ds(pl.multiple_of(at, size), size)]
+
+    def power_to(q, src, u, single):
+        size = rows_each // 2 if single else rows_each
+        return precv_ref.at[q, src, pl.ds(u * size, size)]
+
+    def power_own(q, u, single):
+        src, dst = power_from(q, across, u, single), power_to(q, across, u, single)
+        return load(src, dst, pown_sem.at[q + u])
+
+    def power_arrived(q, u, single):
+        others = power_to(q, pl.ds(0, others_count), u, single)
+        return load(others, others, precv_sem.at[q + u])
+
+    def power_left(q, u, single):
+        others = power_to(q, pl.ds(0, others_count), u, single)
+        return load(others, others, psend_sem.at[q + u])
+
+    def calibrate(q, u, col):
+        volt = recv_ref[q, :, u].reshape(FEEDS, width).astype(jnp.float32)
+        cal = volt * gains_ref[:, :width] + pltpu.roll(volt, chans, 1) * gains_ref[:, width:]
+        turned = pltpu.roll(cal, chans, 1) * sign
+        x_ref[0:FEEDS, col : col + width] = cal.astype(jnp.bfloat16)
+        x_ref[FEEDS : 2 * FEEDS, col : col + width] = turned.astype(jnp.bfloat16)
+
+    def send_powers(q, u, p, single):
+        for dg in range(grp_count - 1, -1, -1):
+            g = (grp + dg) % grp_count
+            here = jnp.logical_and(p == pair, g == grp)
+
+            def go():
+                src = power_from(q, p * grp_count + g, u, single)
+                power_copy(q + u, src, power_to(q, across, u, single), p, g).start()
+
+            if dg:
+                go()
+            else:
+                pl.when(jnp.logical_not(here))(go)
+
+                @pl.when(here)
+                def _():
+                    power_own(q, u, single).start()
 
     def beams(q):
-        arrived(q).wait()
-        own_copy(q).wait()
+        arrived(q, (q,)).wait()
+        own_copy(q, (q,)).wait()
         for u in range(STEP):
-            volt = recv_ref[q, :, u].reshape(FEEDS, width).astype(jnp.float32)
-            cal = volt * gains_ref[:, :width] + pltpu.roll(volt, chans, 1) * gains_ref[:, width:]
-            turned = pltpu.roll(cal, chans, 1) * sign
-            cols = slice(u * width, (u + 1) * width)
-            x_ref[0:FEEDS, cols] = cal.astype(jnp.bfloat16)
-            x_ref[FEEDS : 2 * FEEDS, cols] = turned.astype(jnp.bfloat16)
-        formed = jnp.dot(w_ref[...], x_ref[...], preferred_element_type=jnp.float32)
-        squares = formed * formed
-        one, two = squares[:, :width], squares[:, width:]
-        first = one + pltpu.roll(one, chans, 1)
-        second = two + pltpu.roll(two, chans, 1)
-        power = jnp.where(low, first, second) * (1.0 / FEEDS)
-        psend_ref[q] = power.astype(jnp.bfloat16)
-        for dp in range(pairs - 1, -1, -1):
-            for dg in range(grp_count - 1, -1, -1):
-                if dp == 0 and dg == 0:
-                    power_own(q).start()
-                else:
-                    power_copy(q, (pair + dp) % pairs, (grp + dg) % grp_count).start()
+            calibrate(q, u, u * width)
+
+        def some(h, carry):
+            p = (pair + 1 + h) % pairs
+            rows = pl.ds(pl.multiple_of(p * half, half), half)
+            formed = jnp.dot(w_ref[rows, :], x_ref[...], preferred_element_type=jnp.float32)
+            squares = formed * formed
+            one, two = squares[:, :width], squares[:, width:]
+            first = one + pltpu.roll(one, chans, 1)
+            second = two + pltpu.roll(two, chans, 1)
+            power = jnp.where(low, first, second) * (1.0 / FEEDS)
+            psend_ref[q, rows, :] = power.astype(jnp.bfloat16)
+            send_powers(q, 0, p, False)
+            return carry
+
+        lax.fori_loop(0, pairs, some, 0)
+
+    def beams_single(u):
+        arrived(last + u, (last, u)).wait()
+        own_copy(last + u, (last, u)).wait()
+        calibrate(last, u, 0)
+
+        def some(h, carry):
+            p = (pair + 1 + h) % pairs
+            rows = pl.ds(pl.multiple_of(p * half, half), half)
+            formed = jnp.dot(
+                w_ref[rows, :], x_ref[:, :width], preferred_element_type=jnp.float32
+            )
+            squares = formed * formed
+            power = (squares + pltpu.roll(squares, chans, 1)) * (1.0 / FEEDS)
+            power = power.reshape(grp_count, 2, rows_each // 2, width)
+            lower = low[: rows_each // 2][None]
+            power = jnp.where(lower, power[:, 0], power[:, 1]).reshape(half // 2, width)
+            at = u * half + p * (half // 2)
+            psend_ref[last, pl.ds(pl.multiple_of(at, half // 2), half // 2), :] = power.astype(
+                jnp.bfloat16
+            )
+            send_powers(last, u, p, True)
+            return carry
+
+        lax.fori_loop(0, pairs, some, 0)
+
+    def summed(q, s, rows):
+        both = precv_ref[q, s, rows].astype(jnp.float32)
+        for p in range(1, pairs):
+            both = both + precv_ref[q, p * grp_count + s, rows].astype(jnp.float32)
+        return both
 
     def dedisperse(q):
         for s in range(grp_count):
@@ -630,14 +741,25 @@
                 hit = shift_ref[s * chans : (s + 1) * chans, :] == frame
                 at = (s * STEP + u) * chans
                 t_ref[at : at + chans, :] = jnp.where(hit, HIT, MISS).astype(jnp.bfloat16)
-        power_arrived(q).wait()
-        power_own(q).wait()
+        power_arrived(q, 0, False).wait()
+        power_own(q, 0, False).wait()
         for s in range(grp_count):
-            both = precv_ref[q, s].astype(jnp.float32)
-            for p in range(1, pairs):
-                both = both + precv_ref[q, p * grp_count + s].astype(jnp.float32)
+            both = summed(q, s, slice(None))
             lhs_ref[:, s * width : (s + 1) * width] = both.astype(jnp.bfloat16)
         acc_ref[...] += jnp.dot(lhs_ref[...], t_ref[...], preferred_element_type=jnp.float32)
+
+    def gather_single(u, into_ref):
+        power_arrived(last, u, True).wait()
+        power_own(last, u, True).wait()
+        size = rows_each // 2
+        lower = low[:size]
+        for s in range(0, grp_count, 2):
+            a, b = (summed(last, v, slice(u * size, (u + 1) * size)) for v in (s, s + 1))
+            top = jnp.where(lower, a, pltpu.roll(b, chans, 1))
+            bottom = jnp.where(lower, pltpu.roll(a, chans, 1), b)
+            cols = slice(s * chans, (s + 2) * chans)
+            into_ref[0:size, cols] = top.astype(jnp.bfloat16)
+            into_ref[size : 2 * size, cols] = bottom.astype(jnp.bfloat16)
 
     def body(i, carry):
         @pl.when(i < chunks)
@@ -647,28 +769,37 @@
         @pl.when(i == 1)
         def _():
             fill_gains(gains_ref, gain_table_ref, gain_index_ref, grp, pair)
-            fill_shift(shift_ref, delays_ref, chan_map_ref, mem)
             fill_weights(w_ref, hit_ref, upper_ref, cylinder_ref)
+            fill_shifts(shift_ref, hit_ref, delays_ref, chan_map_ref, mem)
 
         @pl.when(i >= 3)
         def _():
             lax.fori_loop(0, steps, lambda u, c: (dedisperse((i - 3) * steps + u), c)[1], 0)
 
-        @pl.when(jnp.logical_and(i >= 2, i < chunks + 2))
+        @pl.when(i >= 2)
         def _():
-            lax.fori_loop(0, steps, lambda u, c: (beams((i - 2) * steps + u), c)[1], 0)
+            count = jnp.minimum(steps, last - (i - 2) * steps)
+            lax.fori_loop(0, count, lambda u, c: (beams((i - 2) * steps + u), c)[1], 0)
 
         return carry
 
-    lax.fori_loop(0, chunks + 3, body, 0)
-
-    owned = rows_each // mem_count
+    lax.fori_loop(0, chunks + 2, body, 0)
+    beams_single(0)
+    lax.fori_loop((chunks - 1) * steps, last, lambda q, c: (dedisperse(q), c)[1], 0)
+    held = CHANS // mem_count
+    hit = shift_ref[...] == float(TIMES - 2)
+    t_ref[0:held, :] = jnp.where(hit, HIT, MISS).astype(jnp.bfloat16)
+    gather_single(0, part_ref)
+    acc_ref[...] += jnp.dot(part_ref[...], t_ref[0:held, :], preferred_element_type=jnp.float32)
     zsend_ref[...] = acc_ref[...].astype(jnp.bfloat16)
+
+    def owned_rows(m):
+        return pl.ds(pl.multiple_of(m * owned, owned), owned)
 
     def z_copy(d):
         m = (mem + d) % mem_count
         return pltpu.make_async_remote_copy(
-            src_ref=zsend_ref.at[pl.ds(pl.multiple_of(m * owned, owned), owned)],
+            src_ref=zsend_ref.at[owned_rows(m)],
             dst_ref=zrecv_ref.at[d - 1],
             send_sem=zsend_sem.at[d - 1],
             recv_sem=zrecv_sem.at[d - 1],
@@ -676,19 +807,45 @@
             device_id_type=MESH,
         )
 
-    for d in range(1, mem_count):
+    def part_copy(d):
+        m = (mem + d) % mem_count
+        return pltpu.make_async_remote_copy(
+            src_ref=part_ref.at[owned_rows(m)],
+            dst_ref=parts_ref.at[mem],
+            send_sem=lsend_sem.at[d - 1],
+            recv_sem=lrecv_sem.at[d - 1],
+            device_id={"mem": m},
+            device_id_type=MESH,
+        )
+
+    order = sorted(range(1, mem_count), key=lambda d: abs(d - mem_count // 2))
+    for d in order:
         z_copy(d).start()
+    beams_single(1)
 
     def drain(q, carry):
-        left(q).wait()
-        power_left(q).wait()
+        left(q, (q,)).wait()
+        power_left(q, 0, False).wait()
         return carry
 
-    lax.fori_loop(0, chunks * steps, drain, 0)
-    total = acc_ref[pl.ds(pl.multiple_of(mem * owned, owned), owned), :]
-    for d in range(1, mem_count):
+    lax.fori_loop(0, last, drain, 0)
+    gather_single(1, part_ref)
+    for d in order:
+        part_copy(d).start()
+    parts_ref[mem] = part_ref[owned_rows(mem), :]
+    for u in range(STEP):
+        left(last + u, (last, u)).wait()
+        power_left(last, u, True).wait()
+    total = acc_ref[owned_rows(mem), :]
+    for d in order:
         z_copy(d).wait()
         total = total + zrecv_ref[d - 1].astype(jnp.float32)
+    for d in order:
+        part_copy(d).wait()
+    for m in range(mem_count):
+        total = total + jnp.dot(
+            parts_ref[m], hit_ref[m * held : (m + 1) * held, :], preferred_element_type=jnp.float32
+        )
     out_ref[...] = total
 
 
@@ -731,16 +888,12 @@
             pltpu.VMEM((CHANS // mem_count, series), f32),
             pltpu.VMEM((FEEDS, FEEDS), bf16),
             pltpu.VMEM((2, CYL * 16, FEEDS), f32),
+            pltpu.VMEM((rows_each, CHANS // mem_count), bf16),
+            pltpu.VMEM((mem_count, owned, CHANS // mem_count), bf16),
             dma,
             dma((TIMES // GROUP,)),
-            dma((count,)),
-            dma((count,)),
-            dma((count,)),
-            dma((count,)),
-            dma((count,)),
-            dma((count,)),
-            dma((mem_count - 1,)),
-            dma((mem_count - 1,)),
+            *[dma((count - 1 + STEP,))] * 6,
+            *[dma((mem_count - 1,))] * 4,
         ],
         compiler_params=pltpu.CompilerParams(
             collective_id=0, has_side_effects=True, vmem_limit_bytes=FUSED_VMEM * 1024 * 1024

time: 208 us -> 206 us (level)
    pallas_call x1, Pallas kernels: 206 us -> 204 us  [fused_stage(): pl.pallas_call(functools.partial(fused_kernel, sizes), out_shape=jax.Shap...]
where the time goes in v3:
time: 206 us
  Pallas kernels  204 us (99%)
    pallas_call x1, Pallas kernels, fused_stage(): pl.pallas_call(functools.partial(fused_kernel, sizes), out_shape=jax.Shap...  204 us

profile of v3, /device:TPU:0, one launch (start us, length us, event | category | flops | bytes accessed | tf_op | source)
XLA Modules:
  0.0 205.6 jit_solution(12348099801329153999)
XLA Ops:
  0.0 203.7 %shard_map.64 = f32[32,1024]{1,0:T(8,128)} custom-call(f32[64,2,256]{2,1,0:T(2,128)} %gain_table_ref.1, s32[2,1024]{1,0:T(2,128)} %bitcast.5, s32[1,1024]{1,0:T(1,128)} %bitcast.6, s32[32,1024]{1,0:T(8,128)} %delays_ref.1, s32[1,1024]{1,0:T(1,128)} %bitcast.7, bf16[64,71680]{1,0:T(8,128)(2,1)} %bitcast.4), custom_call_target="tpu_custom_call" | custom-call | tf_op jit(solution)/shard_map/pallas_call | solution.py:865
  203.7 1.9 reshape.15

commit v4 on v3

--- a/solution.py
+++ b/solution.py
@@ -304,6 +304,8 @@
 
 GROUP = 4
 STEP = 2
+AHEAD = 1
+WINDOW = 2
 FUSED_VMEM = 62
 
 
@@ -597,18 +599,6 @@
 
         lax.fori_loop(0, chips, tile, 0)
 
-        @pl.when(jnp.logical_and(k > 0, k < chunks - 1))
-        def _():
-            for u in range(steps):
-                post_all(k * steps + u, (k * steps + u,))
-
-        @pl.when(k == chunks - 1)
-        def _():
-            for u in range(steps - 1):
-                post_all(k * steps + u, (k * steps + u,))
-            for u in range(STEP):
-                post_all(last + u, (last, u))
-
     lane = lax.broadcasted_iota(jnp.int32, (FEEDS, width), 1)
     sign = jnp.where(lane < chans, 1.0, -1.0)
     rows_each = BEAMS // (pairs * grp_count)
@@ -762,36 +752,40 @@
             into_ref[size : 2 * size, cols] = bottom.astype(jnp.bfloat16)
 
     def body(i, carry):
-        @pl.when(i < chunks)
+        j = i - AHEAD * steps
+        ready = j + WINDOW
+
+        @pl.when(jnp.logical_and(i % steps == 0, i // steps < chunks))
         def _():
-            dft(i)
-
-        @pl.when(i == 1)
+            dft(i // steps)
+
+        @pl.when(jnp.logical_and(ready >= steps, ready < last))
+        def _():
+            post_all(ready, (ready,))
+
+        @pl.when(jnp.logical_and(ready >= last, ready < last + STEP))
+        def _():
+            post_all(ready, (last, ready - last))
+
+        @pl.when(j == 0)
         def _():
             fill_gains(gains_ref, gain_table_ref, gain_index_ref, grp, pair)
             fill_weights(w_ref, hit_ref, upper_ref, cylinder_ref)
             fill_shifts(shift_ref, hit_ref, delays_ref, chan_map_ref, mem)
 
-        @pl.when(i >= 3)
+        @pl.when(j >= 2)
         def _():
-            lax.fori_loop(0, steps, lambda u, c: (dedisperse((i - 3) * steps + u), c)[1], 0)
-
-        @pl.when(i >= 2)
+            dedisperse(j - 2)
+
+        @pl.when(jnp.logical_and(j >= 0, j < last))
         def _():
-            count = jnp.minimum(steps, last - (i - 2) * steps)
-            lax.fori_loop(0, count, lambda u, c: (beams((i - 2) * steps + u), c)[1], 0)
+            beams(j)
+
+        @pl.when(jnp.logical_and(j >= last, j < last + STEP - 1))
+        def _():
+            beams_single(j - last)
 
         return carry
-
-    lax.fori_loop(0, chunks + 2, body, 0)
-    beams_single(0)
-    lax.fori_loop((chunks - 1) * steps, last, lambda q, c: (dedisperse(q), c)[1], 0)
-    held = CHANS // mem_count
-    hit = shift_ref[...] == float(TIMES - 2)
-    t_ref[0:held, :] = jnp.where(hit, HIT, MISS).astype(jnp.bfloat16)
-    gather_single(0, part_ref)
-    acc_ref[...] += jnp.dot(part_ref[...], t_ref[0:held, :], preferred_element_type=jnp.float32)
-    zsend_ref[...] = acc_ref[...].astype(jnp.bfloat16)
 
     def owned_rows(m):
         return pl.ds(pl.multiple_of(m * owned, owned), owned)
@@ -807,32 +801,55 @@
             device_id_type=MESH,
         )
 
-    def part_copy(d):
+    def part_copy(u, d):
         m = (mem + d) % mem_count
+        at = u * (mem_count - 1) + d - 1
         return pltpu.make_async_remote_copy(
-            src_ref=part_ref.at[owned_rows(m)],
-            dst_ref=parts_ref.at[mem],
-            send_sem=lsend_sem.at[d - 1],
-            recv_sem=lrecv_sem.at[d - 1],
+            src_ref=part_ref.at[u, owned_rows(m)],
+            dst_ref=parts_ref.at[u, mem],
+            send_sem=lsend_sem.at[at],
+            recv_sem=lrecv_sem.at[at],
             device_id={"mem": m},
             device_id_type=MESH,
         )
 
     order = sorted(range(1, mem_count), key=lambda d: abs(d - mem_count // 2))
-    for d in order:
-        z_copy(d).start()
-    beams_single(1)
+
+    def share(u):
+        gather_single(u, part_ref.at[u])
+        for d in order:
+            part_copy(u, d).start()
+        parts_ref[u, mem] = part_ref[u, owned_rows(mem), :]
+
+    def finish(u):
+        for d in order:
+            part_copy(u, d).wait()
+        held = CHANS // mem_count
+        done = None
+        for m in range(mem_count):
+            more = jnp.dot(
+                parts_ref[u, m],
+                hit_ref[m * held : (m + 1) * held, :],
+                preferred_element_type=jnp.float32,
+            )
+            done = more if done is None else done + more
+        return done
 
     def drain(q, carry):
         left(q, (q,)).wait()
         power_left(q, 0, False).wait()
         return carry
 
+    lax.fori_loop(0, AHEAD * steps + last + STEP - 1, body, 0)
+    for q in range(last - 1, last):
+        dedisperse(jnp.int32(q))
+    zsend_ref[...] = acc_ref[...].astype(jnp.bfloat16)
+    for d in order:
+        z_copy(d).start()
+    beams_single(STEP - 1)
+    share(0)
     lax.fori_loop(0, last, drain, 0)
-    gather_single(1, part_ref)
-    for d in order:
-        part_copy(d).start()
-    parts_ref[mem] = part_ref[owned_rows(mem), :]
+    share(1)
     for u in range(STEP):
         left(last + u, (last, u)).wait()
         power_left(last, u, True).wait()
@@ -840,12 +857,12 @@
     for d in order:
         z_copy(d).wait()
         total = total + zrecv_ref[d - 1].astype(jnp.float32)
-    for d in order:
-        part_copy(d).wait()
-    for m in range(mem_count):
-        total = total + jnp.dot(
-            parts_ref[m], hit_ref[m * held : (m + 1) * held, :], preferred_element_type=jnp.float32
-        )
+    before = finish(0)
+    series = before.shape[1]
+    time = iota(before.shape, 1) % TIMES
+    wrapped = pltpu.roll(before, TIMES - 1, 1)
+    total = total + jnp.where(time == TIMES - 1, wrapped, pltpu.roll(before, series - 1, 1))
+    total = total + finish(1)
     out_ref[...] = total
 
 
@@ -888,12 +905,13 @@
             pltpu.VMEM((CHANS // mem_count, series), f32),
             pltpu.VMEM((FEEDS, FEEDS), bf16),
             pltpu.VMEM((2, CYL * 16, FEEDS), f32),
-            pltpu.VMEM((rows_each, CHANS // mem_count), bf16),
-            pltpu.VMEM((mem_count, owned, CHANS // mem_count), bf16),
+            pltpu.VMEM((STEP, rows_each, CHANS // mem_count), bf16),
+            pltpu.VMEM((STEP, mem_count, owned, CHANS // mem_count), bf16),
             dma,
             dma((TIMES // GROUP,)),
             *[dma((count - 1 + STEP,))] * 6,
-            *[dma((mem_count - 1,))] * 4,
+            *[dma((mem_count - 1,))] * 2,
+            *[dma((STEP * (mem_count - 1),))] * 2,
         ],
         compiler_params=pltpu.CompilerParams(
             collective_id=0, has_side_effects=True, vmem_limit_bytes=FUSED_VMEM * 1024 * 1024

time: 206 us -> 204 us (level)
  no operation moved by 1% of the time
where the time goes in v4:
time: 204 us
  Pallas kernels  202 us (99%)
    pallas_call x1, Pallas kernels, fused_stage(): pl.pallas_call(functools.partial(fused_kernel, sizes), out_shape=jax.Shap...  202 us

profile of v4, /device:TPU:0, one launch (start us, length us, event | category | flops | bytes accessed | tf_op | source)
XLA Modules:
  0.0 203.6 jit_solution(16351006216380262080)
XLA Ops:
  0.0 201.7 %shard_map.64 = f32[32,1024]{1,0:T(8,128)} custom-call(f32[64,2,256]{2,1,0:T(2,128)} %gain_table_ref.1, s32[2,1024]{1,0:T(2,128)} %bitcast.5, s32[1,1024]{1,0:T(1,128)} %bitcast.6, s32[32,1024]{1,0:T(8,128)} %delays_ref.1, s32[1,1024]{1,0:T(1,128)} %bitcast.7, bf16[64,71680]{1,0:T(8,128)(2,1)} %bitcast.4), custom_call_target="tpu_custom_call" | custom-call | tf_op jit(solution)/shard_map/pallas_call | solution.py:882
  201.7 1.9 reshape.15

commit v5 on v4

--- a/solution.py
+++ b/solution.py
@@ -541,7 +541,9 @@
 
     def place(s):
         h = s // 2
-        far = (mem + 2) % 4 * ((3 - h) // 3) + (3 - mem) * (h % 3 % 2)
+        one, two = (3 - h) // 3, h % 3 % 2
+        one, two = one + (two - one) * (grp % cores), two + (one - two) * (grp % cores)
+        far = (3 - mem) * one + (mem + 2) % 4 * two
         near = (mem + 1 - 2 * (mem % 2)) * (h % 3 // 2) + mem * (h // 3)
         return (x_here + s + 1) % 2, far + near
 
@@ -549,7 +551,7 @@
         def some(s, carry):
             x, m = place(s)
             for c in range(cores):
-                post(q, at, x * cores + c, m)
+                post(q, at, x * cores + (grp + c) % cores, m)
             return carry
 
         lax.fori_loop(0, chips, some, 0)

time: 204 us -> 203 us (level)
  no operation moved by 1% of the time
where the time goes in v5:
time: 203 us; the launch traced here: 202 us
  Pallas kernels  200 us (99%)
    pallas_call x1, Pallas kernels, fused_stage(): pl.pallas_call(functools.partial(fused_kernel, sizes), out_shape=jax.Shap...  200 us

profile of v5, /device:TPU:0, one launch (start us, length us, event | category | flops | bytes accessed | tf_op | source)
XLA Modules:
  0.0 202.4 jit_solution(1496592258322671445)
XLA Ops:
  0.0 200.5 %shard_map.64 = f32[32,1024]{1,0:T(8,128)} custom-call(f32[64,2,256]{2,1,0:T(2,128)} %gain_table_ref.1, s32[2,1024]{1,0:T(2,128)} %bitcast.5, s32[1,1024]{1,0:T(1,128)} %bitcast.6, s32[32,1024]{1,0:T(8,128)} %delays_ref.1, s32[1,1024]{1,0:T(1,128)} %bitcast.7, bf16[64,71680]{1,0:T(8,128)(2,1)} %bitcast.4), custom_call_target="tpu_custom_call" | custom-call | tf_op jit(solution)/shard_map/pallas_call | solution.py:884
  200.5 1.9 reshape.15

commit v6 on v5

--- a/solution.py
+++ b/solution.py
@@ -824,15 +824,15 @@
         parts_ref[u, mem] = part_ref[u, owned_rows(mem), :]
 
     def finish(u):
-        for d in order:
-            part_copy(u, d).wait()
         held = CHANS // mem_count
         done = None
-        for m in range(mem_count):
+        for d in (0, *order):
+            if d:
+                part_copy(u, d).wait()
+            m = (mem + mem_count - d) % mem_count
+            rows = pl.ds(pl.multiple_of(m * held, held), held)
             more = jnp.dot(
-                parts_ref[u, m],
-                hit_ref[m * held : (m + 1) * held, :],
-                preferred_element_type=jnp.float32,
+                parts_ref[u, m], hit_ref[rows, :], preferred_element_type=jnp.float32
             )
             done = more if done is None else done + more
         return done

time: 203 us -> 202 us (level)
  no operation moved by 1% of the time
where the time goes in v6:
time: 202 us
  Pallas kernels  200 us (99%)
    pallas_call x1, Pallas kernels, fused_stage(): pl.pallas_call(functools.partial(fused_kernel, sizes), out_shape=jax.Shap...  200 us

profile of v6, /device:TPU:0, one launch (start us, length us, event | category | flops | bytes accessed | tf_op | source)
XLA Modules:
  0.0 202.2 jit_solution(338851579458398811)
XLA Ops:
  0.0 200.3 %shard_map.64 = f32[32,1024]{1,0:T(8,128)} custom-call(f32[64,2,256]{2,1,0:T(2,128)} %gain_table_ref.1, s32[2,1024]{1,0:T(2,128)} %bitcast.5, s32[1,1024]{1,0:T(1,128)} %bitcast.6, s32[32,1024]{1,0:T(8,128)} %delays_ref.1, s32[1,1024]{1,0:T(1,128)} %bitcast.7, bf16[64,71680]{1,0:T(8,128)(2,1)} %bitcast.4), custom_call_target="tpu_custom_call" | custom-call | tf_op jit(solution)/shard_map/pallas_call | solution.py:884
  200.3 1.9 reshape.15
